TPU v7x, 512 devices: a whole 4x8x8 slice. The times are simulated.
512 devices in a mesh: blk: 128 (over z, x_lo, y), aux: 4 (over x_hi, core).
Axes of the slice: x: 4 (x_hi: 2, x_lo: 2; x = x_hi * 2 + x_lo), y: 8, z: 8, core: 2. Of those that a mesh axis runs over, the one named last changes fastest.
Arguments:
- ints3c: bfloat16 [8, 65536, 3, 512], P('aux', 'blk'), may hold values from -0.25 to 0.25
- coef: bfloat16 [65536, 256], P('blk'), may hold values from -6 to 6
- tile_mask: int32 [128, 3, 4], P('blk'), may hold values 0 or 1
Outputs:
- band: float32 [65536, 3, 512], P('blk', None, 'aux')
All inputs are finite; a program needn't handle non-finite values. No bound on the sum of `tile_mask` on one device may be relied on, other than what follows from the above.
Results may differ from a plain program's by a relative error of at most 0.0016.
Values may be sent and summed in bfloat16 or wider, within the bound.
No kernel may reach another device: no remote copies, remote signals or barrier semaphores. Data moves between devices by JAX's collectives and lax.ppermute only.
A program may use at most 64 MiB of HBM per device.

v0:
```python
import jax
import jax.numpy as jnp
from jax import lax
from jax.sharding import PartitionSpec as P


def shifted(value, axis, steps):
    count = lax.axis_size(axis)
    pairs = [(source, (source + steps) % count) for source in range(count)]
    return lax.ppermute(value, axis, pairs)


def pair_block(left, right):
    return jnp.einsum("pmki,plki->ml", left, right, preferred_element_type=jnp.float32)


def body(ints3c, coef, tile_mask):
    rows = ints3c.shape[1]
    tiles = tile_mask.shape[2]
    prev_coef = shifted(coef, "blk", 1)
    next_coef = shifted(coef, "blk", -1)
    windows = (prev_coef, coef, next_coef)
    weights = jnp.repeat(tile_mask[0].astype(jnp.float32), rows // tiles, axis=1)
    pieces = [
        jnp.einsum(
            "pmn,ni->pmi", ints3c[:, :, k, :], windows[k], preferred_element_type=jnp.float32
        )
        for k in range(3)
    ]
    half = (jnp.stack(pieces, axis=2) * jnp.transpose(weights)[None, :, :, None]).astype(
        jnp.bfloat16
    )
    diag = pair_block(half, half)
    next_half = shifted(half[:, :, :2], "blk", -1)
    upper = pair_block(half[:, :, 1:], next_half)
    scale = (lax.axis_size("aux") * half.shape[0] * 3 * half.shape[3]) ** (-0.5)
    lower = jnp.transpose(shifted(upper, "blk", 1))
    band = lax.psum_scatter(
        jnp.stack([lower, diag, upper], axis=1), "aux", scatter_dimension=2, tiled=True
    )
    return band * scale


def solution(mesh):
    placed = (P("aux", "blk", None, None), P("blk", None), P("blk", None, None))
    return jax.shard_map(
        body, mesh=mesh, in_specs=placed, out_specs=P("blk", None, "aux"), check_vma=False
    )
```

profile of v0, /device:TPU:1, one launch (start us, length us, event | category | flops | bytes accessed | tf_op | source)
XLA Modules:
  0.0 154.3 jit_solution(9191568485367906417)
XLA Ops:
  6.5 0.0 reduce-scatter.2.cloned.1.call-start
  6.5 4.0 %collective-permute-start = (bf16[512,256]{1,0:T(8,128)(2,1)}, bf16[512,256]{1,0:T(8,128)(2,1)S(1)}, u32[]{:S(2)}, u32[]{:S(2)}) collective-permute-start(bf16[512,256]{1,0:T(8,128)(2,1)} %param.4), channel_id=1, source_target_pairs={{0,4},{4,8},{8,12},{12,16},{16,20},{20,24},{24,28},{28,32},{32,36}... | collective-permute-start | bytes 786440 | tf_op jit(solution)/shard_map/ppermute | solution.py:10
  10.6 13.2 %collective-permute-start.1 = (bf16[512,256]{1,0:T(8,128)(2,1)}, bf16[512,256]{1,0:T(8,128)(2,1)S(1)}, u32[]{:S(2)}, u32[]{:S(2)}) collective-permute-start(bf16[512,256]{1,0:T(8,128)(2,1)} %param.4), channel_id=1, source_target_pairs={{0,508},{4,0},{8,4},{12,8},{16,12},{20,16},{24,20},{28,24},{32,28}... | collective-permute-start | bytes 786440 | tf_op jit(solution)/shard_map/ppermute | solution.py:10
  23.8 0.7 convert_element_type.9
  24.5 0.1 broadcast_bitcast_fusion
  24.6 1.7 %convolution_bitcast_fusion.2 = f32[2,512,1,256]{3,1,0,2:T(8,128)S(1)} fusion(bf16[2,512,3,512]{3,1,2,0:T(8,128)(2,1)} %param.3, bf16[512,256]{1,0:T(8,128)(2,1)} %param.4), kind=kOutput, calls=%fused_computation.5 | convolution fusion | flops 268435456 | bytes 2359296 | tf_op jit(solution)/shard_map/pmn,ni->pmi/dot_general | solution.py:25
  26.3 2.8 %collective-permute-done.1 = bf16[512,256]{1,0:T(8,128)(2,1)S(1)} collective-permute-done((bf16[512,256]{1,0:T(8,128)(2,1)}, bf16[512,256]{1,0:T(8,128)(2,1)S(1)}, u32[]{:S(2)}, u32[]{:S(2)}) %collective-permute-start.1) | collective-permute-done | bytes 262176 | tf_op jit(solution)/shard_map/ppermute | solution.py:10
  29.1 1.7 %convolution_bitcast_fusion.1 = f32[2,512,1,256]{3,1,0,2:T(8,128)S(1)} fusion(bf16[2,512,3,512]{3,1,2,0:T(8,128)(2,1)} %param.3, bf16[512,256]{1,0:T(8,128)(2,1)S(1)} %collective-permute-done.1), kind=kOutput, calls=%fused_computation.4 | convolution fusion | flops 268435456 | bytes 2359296 | tf_op jit(solution)/shard_map/pmn,ni->pmi/dot_general | solution.py:25
  30.7 0.0 collective-permute-done
  30.7 1.7 %convolution_bitcast_fusion.3 = f32[2,512,1,256]{3,1,0,2:T(8,128)S(1)} fusion(bf16[2,512,3,512]{3,1,2,0:T(8,128)(2,1)} %param.3, bf16[512,256]{1,0:T(8,128)(2,1)S(1)} %collective-permute-done), kind=kOutput, calls=%fused_computation.6 | convolution fusion | flops 268435456 | bytes 2359296 | tf_op jit(solution)/shard_map/pmn,ni->pmi/dot_general | solution.py:25
  32.4 0.3 fusion
  32.7 0.1 slice.20
  32.8 8.2 %collective-permute-start.2 = (bf16[2,512,2,256]{3,1,0,2:T(8,128)(2,1)S(1)}, bf16[2,512,2,256]{3,1,0,2:T(8,128)(2,1)S(1)}, u32[]{:S(2)}, u32[]{:S(2)}) collective-permute-start(bf16[2,512,2,256]{3,1,0,2:T(8,128)(2,1)S(1)} %slice.20), channel_id=1, source_target_pairs={{0,508},{4,0},{8,4},{12,8},{16,12},{20,16},{24,20},{28,24},{32,28}... | collective-permute-start | bytes 3145736 | tf_op jit(solution)/shard_map/ppermute | solution.py:10
  41.0 20.9 %collective-permute-done.2 = bf16[2,512,2,256]{3,1,0,2:T(8,128)(2,1)S(1)} collective-permute-done((bf16[2,512,2,256]{3,1,0,2:T(8,128)(2,1)S(1)}, bf16[2,512,2,256]{3,1,0,2:T(8,128)(2,1)S(1)}, u32[]{:S(2)}, u32[]{:S(2)}) %collective-permute-start.2) | collective-permute-done | bytes 1048608 | tf_op jit(solution)/shard_map/ppermute | solution.py:10
  61.9 0.7 fusion.10
  62.6 1.3 copy.7
  63.9 1.9 %collective-permute-start.3 = (f32[512,512]{0,1:T(8,128)}, f32[512,512]{0,1:T(8,128)S(1)}, u32[]{:S(2)}, u32[]{:S(2)}) collective-permute-start(f32[512,512]{0,1:T(8,128)} %copy.7), channel_id=1, source_target_pairs={{0,4},{4,8},{8,12},{12,16},{16,20},{20,24},{24,28},{28,32},{32,36}... | collective-permute-start | bytes 3145736 | tf_op jit(solution)/shard_map/ppermute | solution.py:10
  65.8 1.0 convolution_bitcast_fusion
  66.8 26.6 %collective-permute-done.3 = f32[512,512]{0,1:T(8,128)S(1)} collective-permute-done((f32[512,512]{0,1:T(8,128)}, f32[512,512]{0,1:T(8,128)S(1)}, u32[]{:S(2)}, u32[]{:S(2)}) %collective-permute-start.3) | collective-permute-done | bytes 1048608 | tf_op jit(solution)/shard_map/ppermute | solution.py:10
  93.4 1.9 %pad_maximum_fusion = f32[512,3,512]{2,0,1:T(8,128)} fusion(f32[512,1,512]{2,0,1:T(8,128)S(1)} %bitcast.60, f32[512,1,512]{2,0,1:T(8,128)S(1)} %convolution_bitcast_fusion, f32[512,1,512]{2,0,1:T(8,128)S(1)} %bitcast.61), kind=kLoop, calls=%fused_computation.2 | loop fusion | flops 1572864 | bytes 6291456 | tf_op jit(solution)/shard_map/stack | solution.py:39
  95.4 0.0 reduce-scatter.2.cloned.1.call-update
  95.4 50.0 %reduce-scatter.2.cloned.1.call-done = f32[512,3,128]{2,0,1:T(8,128)} async-done(((f32[512,3,512]{2,0,1:T(8,128)}), f32[512,3,128]{2,0,1:T(8,128)}) %reduce-scatter.2.cloned.1.call-update) | async-done | bytes 786448 | tf_op jit(solution)/shard_map/reduce_scatter | solution.py:38
  145.4 2.1 %broadcast_multiply_fusion = f32[512,3,128]{2,0,1:T(8,128)} fusion(f32[512,3,128]{2,0,1:T(8,128)} %reduce-scatter.2.cloned.1.call-done), kind=kLoop, calls=%fused_computation.13 | loop fusion | flops 196608 | bytes 1572864 | tf_op jit(solution)/shard_map/mul | solution.py:41
  (2 shorter events, 0.0 us)
Async XLA Ops:
  6.5 138.8 %reduce-scatter.2.cloned.1.call-start = ((), (), s32[]{:S(2)}) async-start(), calls=%async_computation.1 | async-start | bytes 3932160 | tf_op jit(solution)/shard_map/reduce_scatter | solution.py:38
  6.5 24.2 %collective-permute-start = (bf16[512,256]{1,0:T(8,128)(2,1)}, bf16[512,256]{1,0:T(8,128)(2,1)S(1)}, u32[]{:S(2)}, u32[]{:S(2)}) collective-permute-start(bf16[512,256]{1,0:T(8,128)(2,1)} %param.4), channel_id=1, source_target_pairs={{0,4},{4,8},{8,12},{12,16},{16,20},{20,24},{24,28},{28,32},{32,36}... | collective-permute-start | bytes 786440 | tf_op jit(solution)/shard_map/ppermute | solution.py:10
  10.6 18.5 %collective-permute-start.1 = (bf16[512,256]{1,0:T(8,128)(2,1)}, bf16[512,256]{1,0:T(8,128)(2,1)S(1)}, u32[]{:S(2)}, u32[]{:S(2)}) collective-permute-start(bf16[512,256]{1,0:T(8,128)(2,1)} %param.4), channel_id=1, source_target_pairs={{0,508},{4,0},{8,4},{12,8},{16,12},{20,16},{24,20},{28,24},{32,28}... | collective-permute-start | bytes 786440 | tf_op jit(solution)/shard_map/ppermute | solution.py:10
  32.8 29.1 %collective-permute-start.2 = (bf16[2,512,2,256]{3,1,0,2:T(8,128)(2,1)S(1)}, bf16[2,512,2,256]{3,1,0,2:T(8,128)(2,1)S(1)}, u32[]{:S(2)}, u32[]{:S(2)}) collective-permute-start(bf16[2,512,2,256]{3,1,0,2:T(8,128)(2,1)S(1)} %slice.20), channel_id=1, source_target_pairs={{0,508},{4,0},{8,4},{12,8},{16,12},{20,16},{24,20},{28,24},{32,28}... | collective-permute-start | bytes 3145736 | tf_op jit(solution)/shard_map/ppermute | solution.py:10
  63.9 29.5 %collective-permute-start.3 = (f32[512,512]{0,1:T(8,128)}, f32[512,512]{0,1:T(8,128)S(1)}, u32[]{:S(2)}, u32[]{:S(2)}) collective-permute-start(f32[512,512]{0,1:T(8,128)} %copy.7), channel_id=1, source_target_pairs={{0,4},{4,8},{8,12},{12,16},{16,20},{20,24},{24,28},{28,32},{32,36}... | collective-permute-start | bytes 3145736 | tf_op jit(solution)/shard_map/ppermute | solution.py:10
Sparse Core Ops, SparseCore 0:
  95.5 49.7 reduce-scatter.1
where the time goes:
time: 155 us; the launch traced here: 154 us
  waiting for transfers between devices  100 us (65%)
  starting transfers between devices  27.4 us (18%)
  between operations  13.5 us (9%)
  matrix products  6.74 us (4%)
  other arithmetic  4.98 us (3%)
    ppermute x4, waiting for transfers between devices, shifted(): return lax.ppermute(value, axis, pairs)  50.3 us
    reduce_scatter x1, waiting for transfers between devices, body(): lax.psum_scatter(jnp.stack([lower, diag, upper], axis=1), 'aux', scatter_...  50 us
    ppermute x4, starting transfers between devices, shifted(): return lax.ppermute(value, axis, pairs)  27.4 us
    dot_general x3, matrix products, body(): jnp.einsum('pmn,ni->pmi', ints3c[:, :, k, :], windows[k], preferred_eleme...  5.01 us
  transfers between devices with their start and end apart: 5, of which 4 were waited for; matrix products, arithmetic and copies ran while one was open for 3% of the time, Pallas kernels for 0%

commit v1 on v0

v1 whole, which is shorter than its diff:
```python
import jax
import jax.numpy as jnp
from jax import lax
from jax.experimental import pallas as pl
from jax.experimental.pallas import tpu as pltpu
from jax.sharding import PartitionSpec as P

F32 = jnp.float32
BF16 = jnp.bfloat16
LIMIT = 8 << 20
MEDIUM = pl.CostEstimate(flops=3_000_000_000, bytes_accessed=1, transcendentals=0)
LARGE = pl.CostEstimate(flops=8_000_000_000, bytes_accessed=1, transcendentals=0)
SMALL = pl.CostEstimate(flops=1, bytes_accessed=1, transcendentals=0)


def dot_rows(left, right):
    return lax.dot_general(left, right, (((1,), (1,)), ((), ())), preferred_element_type=F32)


def weighted_half(mask_ref, k, plane, orbitals, out):
    tiles = mask_ref.shape[-1]
    step = out.shape[0] // tiles
    full = jnp.dot(plane[...], orbitals[...], preferred_element_type=F32)
    for t in range(tiles):
        spot = slice(t * step, (t + 1) * step)
        out[spot, :] = (full[spot] * mask_ref[k, 0, t].astype(F32)).astype(BF16)


def own_kernel(mask_ref, ints, orbitals, out, planes, held, sems):
    per = out.shape[0]
    first = pltpu.make_async_copy(orbitals, held, sems.at[per])
    copies = [
        pltpu.make_async_copy(ints.at[p, 1], planes.at[p], sems.at[p]) for p in range(per)
    ]
    for copy in [first] + copies:
        copy.start()
    first.wait()
    for p in range(per):
        copies[p].wait()
        weighted_half(mask_ref, 1, planes.at[p], held, out.at[p])


def own_middle(mask, ints, orbitals):
    per, _, rows, inner = ints.shape
    cols = orbitals.shape[1]
    hbm = pl.BlockSpec(memory_space=pltpu.HBM)
    return pl.pallas_call(
        own_kernel,
        in_specs=[pl.BlockSpec(memory_space=pltpu.SMEM), hbm, hbm],
        out_specs=pl.BlockSpec(memory_space=pltpu.VMEM),
        out_shape=jax.ShapeDtypeStruct((per, rows, cols), BF16),
        scratch_shapes=[
            pltpu.VMEM((per, rows, inner), BF16),
            pltpu.VMEM((inner, cols), BF16),
            pltpu.SemaphoreType.DMA((per + 1,)),
        ],
        compiler_params=pltpu.CompilerParams(vmem_limit_bytes=LIMIT),
        cost_estimate=SMALL,
        name="own_middle",
    )(mask, ints, orbitals)


def mate_kernel(mask_ref, ints, orbitals, out):
    for p in range(out.shape[0]):
        weighted_half(mask_ref, 1, ints.at[p, 1], orbitals, out.at[p])


def edge_kernel(mask_ref, place_ref, own, mate, orbitals, out, planes, sems):
    side = 2 - 2 * place_ref[0]
    per = planes.shape[0]
    copies = [
        pltpu.make_async_copy(own.at[p, side], planes.at[p], sems.at[p]) for p in range(per)
    ]
    for copy in copies:
        copy.start()
    for p in range(per):
        weighted_half(mask_ref, side, mate.at[p, side], orbitals, out.at[per + p])
    for p in range(per):
        copies[p].wait()
        weighted_half(mask_ref, side, planes.at[p], orbitals, out.at[p])


def edge_half(mask, place, own, mate, orbitals):
    per, _, rows, inner = own.shape
    cols = orbitals.shape[1]
    smem = pl.BlockSpec(memory_space=pltpu.SMEM)
    vmem = pl.BlockSpec(memory_space=pltpu.VMEM)
    return pl.pallas_call(
        edge_kernel,
        in_specs=[smem, smem, pl.BlockSpec(memory_space=pltpu.HBM), vmem, vmem],
        out_specs=vmem,
        out_shape=jax.ShapeDtypeStruct((2 * per, rows, cols), BF16),
        scratch_shapes=[
            pltpu.VMEM((per, rows, inner), BF16),
            pltpu.SemaphoreType.DMA((per,)),
        ],
        compiler_params=pltpu.CompilerParams(vmem_limit_bytes=LIMIT),
        cost_estimate=MEDIUM,
        name="edge_half",
    )(mask, place, own, mate, orbitals)


def diag_kernel(place_ref, edge, own, kept, sent):
    core = place_ref[0]
    rows = edge.shape[1]
    mid = rows // 2
    quarter = mid // 2
    for h in range(2):
        spot = pl.ds(h * mid, mid)
        for r in range(2):
            band = pl.ds(r * mid, mid)
            total = dot_rows(edge[0, band, :], edge[0, spot, :])
            for p in range(1, edge.shape[0]):
                total += dot_rows(edge[p, band, :], edge[p, spot, :])
            for p in range(own.shape[0]):
                total += dot_rows(own[p, band, :], own[p, spot, :])
            first, second = total[:, :quarter], total[:, quarter:]
            kept[h, band, :] = jnp.where(core == 0, first, second)
            sent[h, band, :] = jnp.where(core == 0, second, first)


def near_kernel(edge, near, same, out):
    rows = edge.shape[1]
    per = near.shape[0]
    mid = rows // 2
    for r in range(2):
        band = pl.ds(r * mid, mid)
        total = dot_rows(edge[0, band, :], same[0])
        for p in range(1, per):
            total += dot_rows(edge[p, band, :], same[p])
        for p in range(per):
            total += dot_rows(edge[per + p, band, :], near[p])
        out[band, :] = total


def last_kernel(place_ref, part, own, mate, other, kept, got, mine, theirs):
    far = place_ref[1]
    rows = own.shape[1]
    per = own.shape[0]
    mid = rows // 2
    for r in range(2):
        band = pl.ds(r * mid, mid)
        total = part[band, :]
        for p in range(per):
            total += dot_rows(own[p, band, :], other[per + p])
        for p in range(per):
            total += dot_rows(mate[p, band, :], other[p])
        first, second = total[:, :mid], total[:, mid:]
        mine[band, :mid] = jnp.where(far == 0, first, second)
        theirs[band, :mid] = jnp.where(far == 0, second, first).astype(BF16)
        mine[band, mid:] = kept[far, band, :] + got[far, band, :]
        theirs[band, mid:] = (kept[1 - far, band, :] + got[1 - far, band, :]).astype(BF16)


def whole(kernel, name, outs, *operands, scalars=0, cost=SMALL):
    smem = pl.BlockSpec(memory_space=pltpu.SMEM)
    vmem = pl.BlockSpec(memory_space=pltpu.VMEM)
    return pl.pallas_call(
        kernel,
        in_specs=[smem] * scalars + [vmem] * (len(operands) - scalars),
        out_specs=[vmem] * len(outs),
        out_shape=outs,
        compiler_params=pltpu.CompilerParams(vmem_limit_bytes=LIMIT),
        cost_estimate=cost,
        name=name,
    )(*operands)


def body(ints3c, coef, tile_mask):
    blocks = lax.axis_size("blk")
    group = lax.axis_size("aux")
    aux = lax.axis_index("aux")
    core = aux % 2
    far = aux // 2
    place = jnp.stack([core, far])
    mask = jnp.transpose(tile_mask, (1, 0, 2))

    def device(b, a):
        return (b % blocks) * group + a

    members = [(b, a) for b in range(blocks) for a in range(group)]

    def moved(value, target):
        pairs = [(device(b, a), target(b, a)) for b, a in members]
        return lax.ppermute(value, ("blk", "aux"), pairs)

    def to_edge(value):
        return moved(value, lambda b, a: device(b + 1 - 2 * (a % 2), a ^ 1))

    def to_same(value):
        return moved(value, lambda b, a: device(b - 1 + 2 * (a % 2), a))

    def to_mate(value):
        return moved(value, lambda b, a: device(b, a ^ 1))

    def to_far(value):
        return moved(value, lambda b, a: device(b, a ^ 2))

    def pick(index, first, second):
        return jnp.where(index == 0, first, second)

    ints = jnp.transpose(ints3c, (0, 2, 1, 3))
    per, _, rows, _ = ints.shape
    own_half = own_middle(mask, ints, coef)
    ints, coef, own_half = lax.optimization_barrier((ints, coef, own_half))
    edge_coef = to_edge(coef)
    mate_ints = to_mate(ints)
    near = to_edge(own_half)
    same = to_same(own_half)
    edges = edge_half(mask, place, ints, mate_ints, edge_coef)
    other = to_edge(edges)
    (mate_half,) = whole(
        mate_kernel,
        "mate_middle",
        [jax.ShapeDtypeStruct(own_half.shape, BF16)],
        mask,
        mate_ints,
        coef,
        scalars=1,
    )

    quarter = rows // group
    split = jax.ShapeDtypeStruct((2, rows, quarter), F32)
    kept, sent = whole(
        diag_kernel, "diag", [split, split], place, edges, own_half, scalars=1
    )
    got = to_mate(sent)

    full = jax.ShapeDtypeStruct((rows, rows), F32)
    (part,) = whole(near_kernel, "near", [full], edges, near, same, cost=LARGE)
    width = rows // 2 + quarter
    mine, theirs = whole(
        last_kernel,
        "last",
        [jax.ShapeDtypeStruct((rows, width), F32), jax.ShapeDtypeStruct((rows, width), BF16)],
        place,
        part,
        own_half,
        mate_half,
        other,
        kept,
        got,
        scalars=1,
    )
    scale = (group * per * 3 * own_half.shape[2]) ** (-0.5)
    total = (mine + to_far(theirs).astype(F32)) * scale
    left, right, diag = (total[:, i * quarter : (i + 1) * quarter] for i in range(3))
    kept = pick(core, left, right)
    got = to_mate(pick(core, right, left))
    return jnp.stack([pick(core, got, kept), diag, pick(core, kept, got)], axis=1)


def solution(mesh):
    placed = (P("aux", "blk", None, None), P("blk", None), P("blk", None, None))
    return jax.shard_map(
        body, mesh=mesh, in_specs=placed, out_specs=P("blk", None, "aux"), check_vma=False
    )
```

time: 155 us -> 68.5 us (0.44)
  waiting for transfers between devices: 100 us -> 15.3 us
  between operations: 13.5 us -> 0.18 us
  Pallas kernels: 0 us -> 12.3 us
  starting transfers between devices: 27.4 us -> 38.5 us
  matrix products: 6.74 us -> 0 us
  other arithmetic: 4.98 us -> 1.19 us
    reduce_scatter x1 -> x0, waiting for transfers between devices: 50 us -> none  [body(): lax.psum_scatter(jnp.stack([lower, diag, upper], axis=1), 'aux', scatter_...]
    ppermute x4 -> x8, waiting for transfers between devices: 50.3 us -> 15.3 us  [moved(): return lax.ppermute(value, ('blk', 'aux'), pairs)]
    pallas_call x0 -> x6, Pallas kernels: none -> 12.3 us  [the longest x4 5.91 us: whole(): pl.pallas_call(kernel, in_specs=[smem] * scalars + [vmem] * (len(operands...]
    ppermute x4 -> x8, starting transfers between devices: 27.4 us -> 38.5 us  [moved(): return lax.ppermute(value, ('blk', 'aux'), pairs)]
    dot_general x5 -> x0, matrix products: 6.74 us -> none  [the longest x3 5.01 us: body(): jnp.einsum('pmn,ni->pmi', ints3c[:, :, k, :], windows[k], preferred_eleme...]
    mul x1, other arithmetic: 2.08 us -> 0.09 us  [body(): total = (mine + to_far(theirs).astype(F32)) * scale]
  transfers between devices with their start and end apart: 5 -> 8, of which waited for: 4 -> 3; matrix products, arithmetic and copies ran while one was open for 3% -> 0% of each run, Pallas kernels for 0% -> 12%
where the time goes in v1:
time: 68.5 us; the launch traced here: 68.1 us
  starting transfers between devices  38.5 us (56%)
  waiting for transfers between devices  15.3 us (22%)
  Pallas kernels  12.3 us (18%)
  other arithmetic  1.19 us (2%)
  local copies, waits for them, and re-layouts  0.76 us (1%)
    ppermute x8, starting transfers between devices, moved(): return lax.ppermute(value, ('blk', 'aux'), pairs)  38.5 us
    ppermute x8, waiting for transfers between devices, moved(): return lax.ppermute(value, ('blk', 'aux'), pairs)  15.3 us
    pallas_call x4, Pallas kernels, whole(): pl.pallas_call(kernel, in_specs=[smem] * scalars + [vmem] * (len(operands...  5.91 us
    pallas_call x1, Pallas kernels, edge_half(): pl.pallas_call(edge_kernel, in_specs=[smem, smem, pl.BlockSpec(memory_spa...  3.82 us
    pallas_call x1, Pallas kernels, own_middle(): pl.pallas_call(own_kernel, in_specs=[pl.BlockSpec(memory_space=pltpu.SMEM...  2.55 us
  transfers between devices with their start and end apart: 8, of which 3 were waited for; matrix products, arithmetic and copies ran while one was open for 0% of the time, Pallas kernels for 12%

profile of v1, /device:TPU:1, one launch (start us, length us, event | category | flops | bytes accessed | tf_op | source)
XLA Modules:
  0.0 68.1 jit_solution(15062865541440426147)
XLA Ops:
  0.0 0.8 %copy-done = s32[1,3,4]{2,0,1:T(1,128)S(1)} copy-done((s32[1,3,4]{2,0,1:T(1,128)S(1)}, s32[1,3,4]{2,0,1:T(1,128)}, u32[]{:S(2)}) %copy-start) | copy-done | bytes 72
  0.8 2.5 %own_middle.1.own = bf16[2,512,256]{2,1,0:T(8,128)(2,1)S(1)} custom-call(s32[3,1,4]{2,1,0:T(1,128)S(1)} %bitcast.10, bf16[2,3,512,512]{3,2,1,0:T(8,128)(2,1)} %bitcast.3.ints.own, bf16[512,256]{1,0:T(8,128)(2,1)} %orbitals.2), custom_call_target="tpu_custom_call" | custom-call | flops 1 | bytes 1 | tf_op jit(solution)/shard_map/own_middle/pallas_call | solution.py:47
  3.3 8.8 %collective-permute-start = (bf16[2,3,512,512]{3,2,1,0:T(8,128)(2,1)}, bf16[2,3,512,512]{3,2,1,0:T(8,128)(2,1)}, u32[]{:S(2)}, u32[]{:S(2)}) collective-permute-start(bf16[2,3,512,512]{3,2,1,0:T(8,128)(2,1)} %bitcast.3.ints.own), channel_id=1, source_target_pairs={{0,1},{1,0},{2,3},{3,2},{4,5},{5,4},{6,7},{7,6},{8,9},{9,8},{10,11... | collective-permute-start | bytes 9437192 | tf_op jit(solution)/shard_map/ppermute | solution.py:185
  12.1 9.0 %collective-permute-start.1 = (bf16[512,256]{1,0:T(8,128)(2,1)}, bf16[512,256]{1,0:T(8,128)(2,1)S(1)}, u32[]{:S(2)}, u32[]{:S(2)}) collective-permute-start(bf16[512,256]{1,0:T(8,128)(2,1)} %orbitals.2), channel_id=1, source_target_pairs={{0,5},{1,508},{2,7},{3,510},{4,9},{5,0},{6,11},{7,2},{8,13},{9,4},... | collective-permute-start | bytes 786440 | tf_op jit(solution)/shard_map/ppermute | solution.py:185
  21.1 1.9 %collective-permute-start.3 = (bf16[2,512,256]{2,1,0:T(8,128)(2,1)S(1)}, bf16[2,512,256]{2,1,0:T(8,128)(2,1)S(1)}, u32[]{:S(2)}, u32[]{:S(2)}) collective-permute-start(bf16[2,512,256]{2,1,0:T(8,128)(2,1)S(1)} %own_middle.1.own), channel_id=1, source_target_pairs={{0,508},{1,5},{2,510},{3,7},{4,0},{5,9},{6,2},{7,11},{8,4},{9,13},... | collective-permute-start | bytes 1572872 | tf_op jit(solution)/shard_map/ppermute | solution.py:185
  23.1 4.0 %collective-permute-start.2 = (bf16[2,512,256]{2,1,0:T(8,128)(2,1)S(1)}, bf16[2,512,256]{2,1,0:T(8,128)(2,1)S(1)}, u32[]{:S(2)}, u32[]{:S(2)}) collective-permute-start(bf16[2,512,256]{2,1,0:T(8,128)(2,1)S(1)} %own_middle.1.own), channel_id=1, source_target_pairs={{0,5},{1,508},{2,7},{3,510},{4,9},{5,0},{6,11},{7,2},{8,13},{9,4},... | collective-permute-start | bytes 1572872 | tf_op jit(solution)/shard_map/ppermute | solution.py:185
  27.1 0.1 pad_add_fusion.place_ref
  27.2 0.0 collective-permute-done.1.orbitals
  27.2 0.0 collective-permute-done.mate.ints
  27.2 3.8 %edge_half.1.edge = bf16[4,512,256]{2,1,0:T(8,128)(2,1)S(1)} custom-call(s32[3,1,4]{2,1,0:T(1,128)S(1)} %bitcast.11, s32[2]{0:T(128)S(1)} %pad_add_fusion.place_ref, bf16[2,3,512,512]{3,2,1,0:T(8,128)(2,1)} %bitcast.3.ints.own, bf16[2,3,512,512]{3,2,1,0:T(8,128)(2,1)} %collective-permute-done.mate.ints, bf16[512,256]{1,0:T(8,128)(2,1)S(1)} %collective-permute-done.1.orbitals), custom_call_target="tpu_custom_call" | custom-call | flops 3000000000 | bytes 1 | tf_op jit(solution)/shard_map/edge_half/pallas_call | solution.py:88
  31.0 6.5 %collective-permute-start.4 = (bf16[4,512,256]{2,1,0:T(8,128)(2,1)S(1)}, bf16[4,512,256]{2,1,0:T(8,128)(2,1)S(1)}, u32[]{:S(2)}, u32[]{:S(2)}) collective-permute-start(bf16[4,512,256]{2,1,0:T(8,128)(2,1)S(1)} %edge_half.1.edge), channel_id=1, source_target_pairs={{0,5},{1,508},{2,7},{3,510},{4,9},{5,0},{6,11},{7,2},{8,13},{9,4},... | collective-permute-start | bytes 3145736 | tf_op jit(solution)/shard_map/ppermute | solution.py:185
  37.5 1.5 %diag.1 = (f32[2,512,128]{2,1,0:T(8,128)S(1)}, f32[2,512,128]{2,1,0:T(8,128)S(1)}) custom-call(s32[2]{0:T(128)S(1)} %pad_add_fusion.place_ref, bf16[4,512,256]{2,1,0:T(8,128)(2,1)S(1)} %edge_half.1.edge, bf16[2,512,256]{2,1,0:T(8,128)(2,1)S(1)} %own_middle.1.own), custom_call_target="tpu_custom_call" | custom-call | flops 1 | bytes 1 | tf_op jit(solution)/shard_map/diag/pallas_call | solution.py:158
  39.1 1.9 %collective-permute-start.5 = (f32[2,512,128]{2,1,0:T(8,128)S(1)}, f32[2,512,128]{2,1,0:T(8,128)S(1)}, u32[]{:S(2)}, u32[]{:S(2)}) collective-permute-start(f32[2,512,128]{2,1,0:T(8,128)S(1)} %get-tuple-element.16), channel_id=1, source_target_pairs={{0,1},{1,0},{2,3},{3,2},{4,5},{5,4},{6,7},{7,6},{8,9},{9,8},{10,11... | collective-permute-start | bytes 1572872 | tf_op jit(solution)/shard_map/ppermute | solution.py:185
  41.0 2.3 %mate_middle.1.mate = bf16[2,512,256]{2,1,0:T(8,128)(2,1)S(1)} custom-call(s32[3,1,4]{2,1,0:T(1,128)S(1)} %bitcast.12, bf16[2,3,512,512]{3,2,1,0:T(8,128)(2,1)} %collective-permute-done.mate.ints, bf16[512,256]{1,0:T(8,128)(2,1)} %orbitals.2), custom_call_target="tpu_custom_call" | custom-call | flops 1 | bytes 1 | tf_op jit(solution)/shard_map/mate_middle/pallas_call | solution.py:158
  43.4 0.7 %near.1.part = f32[512,512]{1,0:T(8,128)S(1)} custom-call(bf16[4,512,256]{2,1,0:T(8,128)(2,1)S(1)} %edge_half.1.edge, bf16[2,512,256]{2,1,0:T(8,128)(2,1)S(1)} %collective-permute-done.2.near, bf16[2,512,256]{2,1,0:T(8,128)(2,1)S(1)} %collective-permute-done.3.same), custom_call_target="tpu_custom_call" | custom-call | flops 8000000000 | bytes 1 | tf_op jit(solution)/shard_map/near/pallas_call | solution.py:158
  44.2 8.1 %collective-permute-done.4.other = bf16[4,512,256]{2,1,0:T(8,128)(2,1)S(1)} collective-permute-done((bf16[4,512,256]{2,1,0:T(8,128)(2,1)S(1)}, bf16[4,512,256]{2,1,0:T(8,128)(2,1)S(1)}, u32[]{:S(2)}, u32[]{:S(2)}) %collective-permute-start.4) | collective-permute-done | bytes 1048608 | tf_op jit(solution)/shard_map/ppermute | solution.py:185
  52.2 1.3 %last.1 = (f32[512,384]{1,0:T(8,128)S(1)}, bf16[512,384]{1,0:T(8,128)(2,1)S(1)}) custom-call(s32[2]{0:T(128)S(1)} %pad_add_fusion.place_ref, f32[512,512]{1,0:T(8,128)S(1)} %near.1.part, bf16[2,512,256]{2,1,0:T(8,128)(2,1)S(1)} %own_middle.1.own, bf16[2,512,256]{2,1,0:T(8,128)(2,1)S(1)} %mate_middle.1.mate, ...), custom_call_target="tpu_custom_call" | custom-call | flops 1 | bytes 1 | tf_op jit(solution)/shard_map/last/pallas_call | solution.py:158
  53.5 4.4 %collective-permute-start.6 = (bf16[512,384]{1,0:T(8,128)(2,1)S(1)}, bf16[512,384]{1,0:T(8,128)(2,1)S(1)}, u32[]{:S(2)}, u32[]{:S(2)}) collective-permute-start(bf16[512,384]{1,0:T(8,128)(2,1)S(1)} %get-tuple-element.18), channel_id=1, source_target_pairs={{0,2},{1,3},{2,0},{3,1},{4,6},{5,7},{6,4},{7,5},{8,10},{9,11},{10,... | collective-permute-start | bytes 1179656 | tf_op jit(solution)/shard_map/ppermute | solution.py:185
  57.9 5.7 %collective-permute-done.6 = bf16[512,384]{1,0:T(8,128)(2,1)S(1)} collective-permute-done((bf16[512,384]{1,0:T(8,128)(2,1)S(1)}, bf16[512,384]{1,0:T(8,128)(2,1)S(1)}, u32[]{:S(2)}, u32[]{:S(2)}) %collective-permute-start.6) | collective-permute-done | bytes 393248 | tf_op jit(solution)/shard_map/ppermute | solution.py:185
  63.6 0.1 add_multiply_fusion
  63.7 1.9 %collective-permute-start.7 = (f32[512,128]{1,0:T(8,128)S(1)}, f32[512,128]{1,0:T(8,128)S(1)}, u32[]{:S(2)}, u32[]{:S(2)}) collective-permute-start(f32[512,128]{1,0:T(8,128)S(1)} %slice_select_fusion.1), channel_id=1, source_target_pairs={{0,1},{1,0},{2,3},{3,2},{4,5},{5,4},{6,7},{7,6},{8,9},{9,8},{10,11... | collective-permute-start | bytes 786440 | tf_op jit(solution)/shard_map/ppermute | solution.py:185
  65.6 1.5 %collective-permute-done.7 = f32[512,128]{1,0:T(8,128)S(1)} collective-permute-done((f32[512,128]{1,0:T(8,128)S(1)}, f32[512,128]{1,0:T(8,128)S(1)}, u32[]{:S(2)}, u32[]{:S(2)}) %collective-permute-start.7) | collective-permute-done | bytes 262176 | tf_op jit(solution)/shard_map/ppermute | solution.py:185
  67.1 0.1 select_bitcast_fusion.1
  67.2 0.9 %pad_maximum_fusion = f32[512,3,128]{2,0,1:T(8,128)} fusion(f32[512,1,128]{2,0,1:T(8,128)S(1)} %get-tuple-element.20, f32[512,1,128]{2,0,1:T(8,128)S(1)} %get-tuple-element.21, f32[512,1,128]{2,0,1:T(8,128)S(1)} %get-tuple-element.19), kind=kLoop, calls=%fused_computation | loop fusion | flops 393216 | bytes 1572864 | tf_op jit(solution)/shard_map/stack | solution.py:250
  (7 shorter events, 0.0 us)
Async XLA Ops:
  0.0 27.2 %copy-start.1 = (s32[1,3,4]{2,0,1:T(1,128)S(1)}, s32[1,3,4]{2,0,1:T(1,128)}, u32[]{:S(2)}) copy-start(s32[1,3,4]{2,0,1:T(1,128)} %param.5) | copy-start | bytes 148
  0.0 0.8 %copy-start = (s32[1,3,4]{2,0,1:T(1,128)S(1)}, s32[1,3,4]{2,0,1:T(1,128)}, u32[]{:S(2)}) copy-start(s32[1,3,4]{2,0,1:T(1,128)} %param.5) | copy-start | bytes 148
  3.3 23.9 %collective-permute-start = (bf16[2,3,512,512]{3,2,1,0:T(8,128)(2,1)}, bf16[2,3,512,512]{3,2,1,0:T(8,128)(2,1)}, u32[]{:S(2)}, u32[]{:S(2)}) collective-permute-start(bf16[2,3,512,512]{3,2,1,0:T(8,128)(2,1)} %bitcast.3.ints.own), channel_id=1, source_target_pairs={{0,1},{1,0},{2,3},{3,2},{4,5},{5,4},{6,7},{7,6},{8,9},{9,8},{10,11... | collective-permute-start | bytes 9437192 | tf_op jit(solution)/shard_map/ppermute | solution.py:185
  12.1 15.1 %collective-permute-start.1 = (bf16[512,256]{1,0:T(8,128)(2,1)}, bf16[512,256]{1,0:T(8,128)(2,1)S(1)}, u32[]{:S(2)}, u32[]{:S(2)}) collective-permute-start(bf16[512,256]{1,0:T(8,128)(2,1)} %orbitals.2), channel_id=1, source_target_pairs={{0,5},{1,508},{2,7},{3,510},{4,9},{5,0},{6,11},{7,2},{8,13},{9,4},... | collective-permute-start | bytes 786440 | tf_op jit(solution)/shard_map/ppermute | solution.py:185
  21.1 22.2 %collective-permute-start.3 = (bf16[2,512,256]{2,1,0:T(8,128)(2,1)S(1)}, bf16[2,512,256]{2,1,0:T(8,128)(2,1)S(1)}, u32[]{:S(2)}, u32[]{:S(2)}) collective-permute-start(bf16[2,512,256]{2,1,0:T(8,128)(2,1)S(1)} %own_middle.1.own), channel_id=1, source_target_pairs={{0,508},{1,5},{2,510},{3,7},{4,0},{5,9},{6,2},{7,11},{8,4},{9,13},... | collective-permute-start | bytes 1572872 | tf_op jit(solution)/shard_map/ppermute | solution.py:185
  23.1 20.3 %collective-permute-start.2 = (bf16[2,512,256]{2,1,0:T(8,128)(2,1)S(1)}, bf16[2,512,256]{2,1,0:T(8,128)(2,1)S(1)}, u32[]{:S(2)}, u32[]{:S(2)}) collective-permute-start(bf16[2,512,256]{2,1,0:T(8,128)(2,1)S(1)} %own_middle.1.own), channel_id=1, source_target_pairs={{0,5},{1,508},{2,7},{3,510},{4,9},{5,0},{6,11},{7,2},{8,13},{9,4},... | collective-permute-start | bytes 1572872 | tf_op jit(solution)/shard_map/ppermute | solution.py:185
  31.0 21.2 %collective-permute-start.4 = (bf16[4,512,256]{2,1,0:T(8,128)(2,1)S(1)}, bf16[4,512,256]{2,1,0:T(8,128)(2,1)S(1)}, u32[]{:S(2)}, u32[]{:S(2)}) collective-permute-start(bf16[4,512,256]{2,1,0:T(8,128)(2,1)S(1)} %edge_half.1.edge), channel_id=1, source_target_pairs={{0,5},{1,508},{2,7},{3,510},{4,9},{5,0},{6,11},{7,2},{8,13},{9,4},... | collective-permute-start | bytes 3145736 | tf_op jit(solution)/shard_map/ppermute | solution.py:185
  39.1 5.0 %collective-permute-start.5 = (f32[2,512,128]{2,1,0:T(8,128)S(1)}, f32[2,512,128]{2,1,0:T(8,128)S(1)}, u32[]{:S(2)}, u32[]{:S(2)}) collective-permute-start(f32[2,512,128]{2,1,0:T(8,128)S(1)} %get-tuple-element.16), channel_id=1, source_target_pairs={{0,1},{1,0},{2,3},{3,2},{4,5},{5,4},{6,7},{7,6},{8,9},{9,8},{10,11... | collective-permute-start | bytes 1572872 | tf_op jit(solution)/shard_map/ppermute | solution.py:185
  53.5 10.0 %collective-permute-start.6 = (bf16[512,384]{1,0:T(8,128)(2,1)S(1)}, bf16[512,384]{1,0:T(8,128)(2,1)S(1)}, u32[]{:S(2)}, u32[]{:S(2)}) collective-permute-start(bf16[512,384]{1,0:T(8,128)(2,1)S(1)} %get-tuple-element.18), channel_id=1, source_target_pairs={{0,2},{1,3},{2,0},{3,1},{4,6},{5,7},{6,4},{7,5},{8,10},{9,11},{10,... | collective-permute-start | bytes 1179656 | tf_op jit(solution)/shard_map/ppermute | solution.py:185
  63.7 3.4 %collective-permute-start.7 = (f32[512,128]{1,0:T(8,128)S(1)}, f32[512,128]{1,0:T(8,128)S(1)}, u32[]{:S(2)}, u32[]{:S(2)}) collective-permute-start(f32[512,128]{1,0:T(8,128)S(1)} %slice_select_fusion.1), channel_id=1, source_target_pairs={{0,1},{1,0},{2,3},{3,2},{4,5},{5,4},{6,7},{7,6},{8,9},{9,8},{10,11... | collective-permute-start | bytes 786440 | tf_op jit(solution)/shard_map/ppermute | solution.py:185

commit v2 on v0

v2 whole, which is shorter than its diff:
```python
import jax
import jax.numpy as jnp
from jax import lax
from jax.experimental import pallas as pl
from jax.experimental.pallas import tpu as pltpu
from jax.sharding import PartitionSpec as P

F32 = jnp.float32
BF16 = jnp.bfloat16
LIMIT = 8 << 20
SMEM = pl.BlockSpec(memory_space=pltpu.SMEM)
VMEM = pl.BlockSpec(memory_space=pltpu.VMEM)
HBM = pl.BlockSpec(memory_space=pltpu.HBM)


def call(kernel, name, specs, outs, operands, scratch=(), cost=1, out_specs=None, aliases=None):
    return pl.pallas_call(
        kernel,
        in_specs=specs,
        out_specs=[VMEM] * len(outs) if out_specs is None else out_specs,
        out_shape=outs,
        scratch_shapes=scratch,
        input_output_aliases=aliases or {},
        compiler_params=pltpu.CompilerParams(vmem_limit_bytes=LIMIT),
        cost_estimate=pl.CostEstimate(flops=int(cost), bytes_accessed=1, transcendentals=0),
        name=name,
    )(*operands)


def in_hbm(value):
    return pltpu.with_memory_space_constraint(value, pltpu.HBM)


def dot_rows(left, right):
    return lax.dot_general(left, right, (((1,), (1,)), ((), ())), preferred_element_type=F32)


def weighted(mask_ref, k, first, plane, orbitals):
    full = jnp.dot(plane[...], orbitals[...], preferred_element_type=F32)
    step = 128
    tiles = [
        full[t * step : (t + 1) * step] * mask_ref[k, 0, first + t].astype(F32)
        for t in range(full.shape[0] // step)
    ]
    return jnp.concatenate(tiles, axis=0).astype(BF16)


def sides():
    aux = lax.axis_index("aux")
    return lax.rem(aux, 2), lax.div(aux, 2)


def own_kernel(mask, ints, orbitals, out, held, mask_ref, planes, sems):
    per = out.shape[0]
    copies = [
        pltpu.make_async_copy(ints.at[p, 1], planes.at[p], sems.at[p]) for p in range(per)
    ]
    copies.append(pltpu.make_async_copy(orbitals, held, sems.at[per]))
    copies.append(pltpu.make_async_copy(mask, mask_ref, sems.at[per + 1]))
    for i in (per, 0, per + 1, *range(1, per)):
        copies[i].start()
    copies[per].wait()
    copies[per + 1].wait()
    for p in range(per):
        copies[p].wait()
        out[p] = weighted(mask_ref, 1, 0, planes.at[p], held)


def mate_kernel(mask, ints, orbitals, out, mask_ref, planes, sems):
    per = out.shape[0]
    copies = [
        pltpu.make_async_copy(ints.at[p, 1], planes.at[p], sems.at[p]) for p in range(per)
    ]
    copies.append(pltpu.make_async_copy(mask, mask_ref, sems.at[per]))
    for copy in copies:
        copy.start()
    copies[per].wait()
    for p in range(per):
        copies[p].wait()
        out[p] = weighted(mask_ref, 1, 0, planes.at[p], orbitals)


def spot(part, size):
    return pl.ds(pl.multiple_of(part * size, size), size)


def edge_kernel(mask, own, mate, orbitals, away, home, mask_ref, planes, sems):
    core, far = sides()
    side = 2 - 2 * core
    count, rows, _ = planes.shape
    per = count // 2
    mid = rows // 2
    copies = []
    for p in range(count):
        source = own.at[p, side] if p < per else mate.at[p - per, side]
        copies.append(pltpu.make_async_copy(source, planes.at[p], sems.at[p]))
    copies.append(pltpu.make_async_copy(mask, mask_ref, sems.at[count]))
    for copy in copies:
        copy.start()
    copies[count].wait()
    for p in range(count):
        copies[p].wait()
        for out, part in ((away, 1 - far), (home, far)):
            plane = planes.at[p, spot(part, mid)]
            out[p] = weighted(mask_ref, side, 2 * part, plane, orbitals)


def product(left, right):
    total = dot_rows(left[0][...], right[0][...])
    for i in range(1, len(left)):
        total += dot_rows(left[i][...], right[i][...])
    return total


def planes_of(ref, count, rows):
    return [ref.at[p, rows] for p in range(count)]


def diag_kernel(away, home, own, kept, sent):
    core, far = sides()
    count, mid, _ = away.shape
    per = own.shape[0]
    quarter = mid // 2
    every = pl.ds(0, mid)
    parts = ((1 - far, away), (far, home))
    for part, right in parts:
        rights = planes_of(right, count, every) + planes_of(own, per, spot(part, mid))
        for band, left in parts:
            rows = spot(band, mid)
            total = product(planes_of(left, count, every) + planes_of(own, per, rows), rights)
            first, second = total[:, :quarter], total[:, quarter:]
            kept[part, rows, :] = jnp.where(core == 0, first, second)
            sent[part, rows, :] = jnp.where(core == 0, second, first)


def block_rows(far, part, away, home, same, near, own, mate, other):
    count, mid, _ = away.shape
    per = own.shape[0]
    every = pl.ds(0, mid)
    cols = spot(part, mid)
    right = planes_of(same, per, cols) + planes_of(near, per, cols)
    right += [other.at[per + p] for p in range(per)] + [other.at[p] for p in range(per)]
    for band, left in ((1 - far, away), (far, home)):
        rows = spot(band, mid)
        lefts = planes_of(left, count, every)
        lefts += planes_of(own, per, rows) + planes_of(mate, per, rows)
        yield rows, product(lefts, right)


def away_kernel(
    away, home, same, near, own, mate, other, kept, got, straight, crossed
):
    core, far = sides()
    width = crossed.shape[1]
    for rows, total in block_rows(far, 1 - far, away, home, same, near, own, mate, other):
        first, second = total[:, :width], total[:, width:]
        straight[rows, :width] = jnp.where(core == 0, first, second).astype(BF16)
        crossed[rows, :] = jnp.where(core == 0, second, first).astype(BF16)
        straight[rows, width:] = (kept[1 - far, rows, :] + got[1 - far, rows, :]).astype(BF16)


def home_kernel(away, home, same, near, own, mate, other, kept, got, held, sent):
    core, far = sides()
    width = sent.shape[1]
    for rows, total in block_rows(far, far, away, home, same, near, own, mate, other):
        first, second = total[:, :width], total[:, width:]
        held[0, rows, :] = jnp.where(core == 0, first, second)
        held[1, rows, :] = kept[far, rows, :] + got[far, rows, :]
        sent[rows, :] = jnp.where(core == 0, second, first)


def settle_kernel(scale, kept, straight, crossed, out, cross, held, sems):
    core, _ = sides()
    width = crossed.shape[1]
    copies = []
    for i, place in enumerate((2 - 2 * core, 1)):
        held[i] = (kept[i] + straight[:, i * width : (i + 1) * width].astype(F32)) * scale
        copies.append(pltpu.make_async_copy(held.at[i], out.at[place], sems.at[i]))
        copies[i].start()
    cross[...] = crossed[...]
    for copy in copies:
        copy.wait()


def band_kernel(scale, got, cross, band, out, held, sems):
    core, _ = sides()
    held[...] = (got[...] + cross[...].astype(F32)) * scale
    copy = pltpu.make_async_copy(held, out.at[2 * core], sems.at[0])
    copy.start()
    copy.wait()


def body(ints3c, coef, tile_mask):
    blocks = lax.axis_size("blk")
    group = lax.axis_size("aux")
    mask = jnp.transpose(tile_mask, (1, 0, 2))
    ints = jnp.transpose(ints3c, (0, 2, 1, 3))
    mask, coef, ints = in_hbm(mask), in_hbm(coef), in_hbm(ints)
    per, _, rows, inner = ints.shape
    cols = coef.shape[1]
    mid, quarter = rows // 2, rows // group

    def device(b, a):
        return (b % blocks) * group + a

    members = [(b, a) for b in range(blocks) for a in range(group)]

    def moved(value, target):
        pairs = [(device(b, a), target(b, a)) for b, a in members]
        return lax.ppermute(value, ("blk", "aux"), pairs)

    def to_edge(value):
        return moved(value, lambda b, a: device(b + 1 - 2 * (a % 2), a ^ 1))

    def to_same(value):
        return moved(value, lambda b, a: device(b - 1 + 2 * (a % 2), a))

    def within(value, flip):
        return moved(value, lambda b, a: device(b, a ^ flip))

    half = jax.ShapeDtypeStruct((per, rows, cols), BF16)
    smem = pltpu.SMEM(mask.shape, mask.dtype)
    planes = pltpu.VMEM((per, rows, inner), BF16)
    own_half, coef = call(
        own_kernel,
        "own_middle",
        [HBM, HBM, HBM],
        [half, jax.ShapeDtypeStruct(coef.shape, BF16)],
        (mask, ints, coef),
        [smem, planes, pltpu.SemaphoreType.DMA((per + 2,))],
    )
    ints, own_half = lax.optimization_barrier((ints, own_half))
    ints = in_hbm(ints)
    edge_coef = to_edge(coef)
    mate_ints = in_hbm(within(ints, 1))
    same = to_same(own_half)
    near = to_edge(own_half)
    part = jax.ShapeDtypeStruct((2 * per, mid, cols), BF16)
    away, home = call(
        edge_kernel,
        "edge_half",
        [HBM, HBM, HBM, VMEM],
        [part, part],
        (mask, ints, mate_ints, edge_coef),
        [
            smem,
            pltpu.VMEM((2 * per, rows, inner), BF16),
            pltpu.SemaphoreType.DMA((2 * per + 1,)),
        ],
        cost=COSTS["edge"],
    )
    other_away = to_edge(away)
    (mate_half,) = call(
        mate_kernel,
        "mate_middle",
        [HBM, HBM, VMEM],
        [half],
        (mask, mate_ints, coef),
        [smem, planes, pltpu.SemaphoreType.DMA((per + 1,))],
        cost=COSTS["mate"],
    )

    pair = jax.ShapeDtypeStruct((2, rows, quarter), F32)
    kept, sent = call(
        diag_kernel,
        "diag",
        [VMEM] * 3,
        [pair, pair],
        (away, home, own_half),
        cost=COSTS["diag"],
    )
    got = within(sent, 1)
    late, kept = lax.optimization_barrier((home, kept))
    other_home = to_edge(late)

    shared = (away, home, same, near, own_half, mate_half)
    quarters = jax.ShapeDtypeStruct((rows, quarter), BF16)
    straight, crossed = call(
        away_kernel,
        "away",
        [VMEM] * 9,
        [jax.ShapeDtypeStruct((rows, mid), BF16), quarters],
        shared + (other_away, kept, got),
        cost=COSTS["away"],
    )
    straight = within(straight, 2)
    crossed = within(crossed, 3)
    held, sent = call(
        home_kernel,
        "home",
        [VMEM] * 9,
        [pair, jax.ShapeDtypeStruct((rows, quarter), F32)],
        shared + (other_home, kept, got),
        cost=COSTS["home"],
    )
    got = within(sent, 1)
    scale = (group * per * 3 * cols) ** (-0.5)
    whole = jax.ShapeDtypeStruct((3, rows, quarter), F32)
    band, cross = call(
        lambda *refs: settle_kernel(scale, *refs),
        "settle",
        [VMEM] * 3,
        [whole, quarters],
        (held, straight, crossed),
        [pltpu.VMEM((2, rows, quarter), F32), pltpu.SemaphoreType.DMA((2,))],
        out_specs=[HBM, VMEM],
        cost=COSTS["settle"],
    )
    (band,) = call(
        lambda *refs: band_kernel(scale, *refs),
        "band",
        [VMEM, VMEM, HBM],
        [whole],
        (got, cross, band),
        [pltpu.VMEM((rows, quarter), F32), pltpu.SemaphoreType.DMA((1,))],
        out_specs=[HBM],
        aliases={2: 0},
    )
    return jnp.transpose(band, (1, 0, 2))


COSTS = {"edge": 3e9, "diag": 1, "mate": 8e9, "away": 8e9, "home": 1, "settle": 8e9}


def solution(mesh):
    placed = (P("aux", "blk", None, None), P("blk", None), P("blk", None, None))
    return jax.shard_map(
        body, mesh=mesh, in_specs=placed, out_specs=P("blk", None, "aux"), check_vma=False
    )
```

time: 155 us -> 62.7 us (0.40)
  waiting for transfers between devices: 100 us -> 5.25 us
  starting transfers between devices: 27.4 us -> 44.5 us
  between operations: 13.5 us -> 0.2 us
  Pallas kernels: 0 us -> 10.6 us
  matrix products: 6.74 us -> 0 us
  other arithmetic: 4.98 us -> 0 us
    reduce_scatter x1 -> x0, waiting for transfers between devices: 50 us -> none  [body(): lax.psum_scatter(jnp.stack([lower, diag, upper], axis=1), 'aux', scatter_...]
    ppermute x4 -> x10, waiting for transfers between devices: 50.3 us -> 5.25 us  [moved(): return lax.ppermute(value, ('blk', 'aux'), pairs)]
    ppermute x4 -> x10, starting transfers between devices: 27.4 us -> 44.5 us  [moved(): return lax.ppermute(value, ('blk', 'aux'), pairs)]
    pallas_call x0 -> x8, Pallas kernels: none -> 10.6 us  [call(): pl.pallas_call(kernel, in_specs=specs, out_specs=[VMEM] * len(outs) if ou...]
    dot_general x5 -> x0, matrix products: 6.74 us -> none  [the longest x3 5.01 us: body(): jnp.einsum('pmn,ni->pmi', ints3c[:, :, k, :], windows[k], preferred_eleme...]
    mul x1 -> x0, other arithmetic: 2.08 us -> none  [body(): return band * scale]
    another operation x1 -> x0, other arithmetic: 1.95 us -> none  [body(): jnp.stack([lower, diag, upper], axis=1)]
    unnamed x3 -> x4, local copies, waits for them, and re-layouts: 0.08 us -> 1.77 us
  transfers between devices with their start and end apart: 5 -> 10, of which waited for: 4 -> 2; matrix products, arithmetic and copies ran while one was open for 3% -> 0% of each run, Pallas kernels for 0% -> 12%
where the time goes in v2:
time: 62.7 us; the launch traced here: 62.3 us
  starting transfers between devices  44.5 us (71%)
  Pallas kernels  10.6 us (17%)
  waiting for transfers between devices  5.25 us (8%)
  local copies, waits for them, and re-layouts  1.77 us (3%)
    ppermute x10, starting transfers between devices, moved(): return lax.ppermute(value, ('blk', 'aux'), pairs)  44.5 us
    pallas_call x8, Pallas kernels, call(): pl.pallas_call(kernel, in_specs=specs, out_specs=[VMEM] * len(outs) if ou...  10.6 us
    ppermute x10, waiting for transfers between devices, moved(): return lax.ppermute(value, ('blk', 'aux'), pairs)  5.25 us
    unnamed x4, local copies, waits for them, and re-layouts  1.77 us
  transfers between devices with their start and end apart: 10, of which 2 were waited for; matrix products, arithmetic and copies ran while one was open for 0% of the time, Pallas kernels for 12%

profile of v2, /device:TPU:1, one launch (start us, length us, event | category | flops | bytes accessed | tf_op | source)
XLA Modules:
  0.0 62.3 jit_solution(1787698389724814275)
XLA Ops:
  0.0 2.1 %own_middle.1 = (bf16[2,512,256]{2,1,0:T(8,128)(2,1)S(1)}, bf16[512,256]{1,0:T(8,128)(2,1)S(1)}) custom-call(s32[3,1,4]{2,1,0:T(1,128)} %bitcast.6, bf16[2,3,512,512]{3,2,1,0:T(8,128)(2,1)} %bitcast.3, bf16[512,256]{1,0:T(8,128)(2,1)} %orbitals.1), custom_call_target="tpu_custom_call" | custom-call | flops 1 | bytes 1 | tf_op jit(solution)/shard_map/own_middle/pallas_call | solution.py:17
  2.2 0.1 copy-done
  2.3 8.8 %collective-permute-start = (bf16[2,3,512,512]{3,2,1,0:T(8,128)(2,1)S(1)}, bf16[2,3,512,512]{3,2,1,0:T(8,128)(2,1)S(1)}, u32[]{:S(2)}, u32[]{:S(2)}) collective-permute-start(bf16[2,3,512,512]{3,2,1,0:T(8,128)(2,1)S(1)} %bitcast.5), channel_id=1, source_target_pairs={{0,1},{1,0},{2,3},{3,2},{4,5},{5,4},{6,7},{7,6},{8,9},{9,8},{10,11... | collective-permute-start | bytes 9437192 | tf_op jit(solution)/shard_map/ppermute | solution.py:210
  11.1 9.0 %collective-permute-start.1 = (bf16[512,256]{1,0:T(8,128)(2,1)S(1)}, bf16[512,256]{1,0:T(8,128)(2,1)S(1)}, u32[]{:S(2)}, u32[]{:S(2)}) collective-permute-start(bf16[512,256]{1,0:T(8,128)(2,1)S(1)} %get-tuple-element.23.orbitals), channel_id=1, source_target_pairs={{0,5},{1,508},{2,7},{3,510},{4,9},{5,0},{6,11},{7,2},{8,13},{9,4},... | collective-permute-start | bytes 786440 | tf_op jit(solution)/shard_map/ppermute | solution.py:210
  20.1 1.9 %collective-permute-start.2 = (bf16[2,512,256]{2,1,0:T(8,128)(2,1)S(1)}, bf16[2,512,256]{2,1,0:T(8,128)(2,1)S(1)}, u32[]{:S(2)}, u32[]{:S(2)}) collective-permute-start(bf16[2,512,256]{2,1,0:T(8,128)(2,1)S(1)} %get-tuple-element.26.own), channel_id=1, source_target_pairs={{0,508},{1,5},{2,510},{3,7},{4,0},{5,9},{6,2},{7,11},{8,4},{9,13},... | collective-permute-start | bytes 1572872 | tf_op jit(solution)/shard_map/ppermute | solution.py:210
  22.0 4.0 %collective-permute-start.3 = (bf16[2,512,256]{2,1,0:T(8,128)(2,1)S(1)}, bf16[2,512,256]{2,1,0:T(8,128)(2,1)S(1)}, u32[]{:S(2)}, u32[]{:S(2)}) collective-permute-start(bf16[2,512,256]{2,1,0:T(8,128)(2,1)S(1)} %get-tuple-element.26.own), channel_id=1, source_target_pairs={{0,5},{1,508},{2,7},{3,510},{4,9},{5,0},{6,11},{7,2},{8,13},{9,4},... | collective-permute-start | bytes 1572872 | tf_op jit(solution)/shard_map/ppermute | solution.py:210
  26.1 0.0 collective-permute-done.mate.ints
  26.1 1.6 %copy-done.1 = bf16[2,3,512,512]{3,2,1,0:T(8,128)(2,1)} copy-done((bf16[2,3,512,512]{3,2,1,0:T(8,128)(2,1)}, bf16[2,3,512,512]{3,2,1,0:T(8,128)(2,1)S(1)}, u32[]{:S(2)}) %copy-start.1) | copy-done | bytes 3145752
  27.7 2.3 %edge_half.1 = (bf16[4,256,256]{2,1,0:T(8,128)(2,1)S(1)}, bf16[4,256,256]{2,1,0:T(8,128)(2,1)S(1)}) custom-call(s32[3,1,4]{2,1,0:T(1,128)} %bitcast.7, bf16[2,3,512,512]{3,2,1,0:T(8,128)(2,1)} %bitcast.4, bf16[2,3,512,512]{3,2,1,0:T(8,128)(2,1)} %copy-done.1, bf16[512,256]{1,0:T(8,128)(2,1)S(1)} %collective-permute-done.1.orbitals), custom_call_target="tpu_custom_call" | custom-call | flops 3000000000 | bytes 1 | tf_op jit(solution)/shard_map/edge_half/pallas_call | solution.py:17
  30.0 6.2 %collective-permute-start.7 = (bf16[4,256,256]{2,1,0:T(8,128)(2,1)S(1)}, bf16[4,256,256]{2,1,0:T(8,128)(2,1)S(1)}, u32[]{:S(2)}, u32[]{:S(2)}) collective-permute-start(bf16[4,256,256]{2,1,0:T(8,128)(2,1)S(1)} %get-tuple-element.24.away), channel_id=1, source_target_pairs={{0,5},{1,508},{2,7},{3,510},{4,9},{5,0},{6,11},{7,2},{8,13},{9,4},... | collective-permute-start | bytes 1572872 | tf_op jit(solution)/shard_map/ppermute | solution.py:210
  36.2 1.0 %diag.1 = (f32[2,512,128]{2,1,0:T(8,128)S(1)}, f32[2,512,128]{2,1,0:T(8,128)S(1)}) custom-call(bf16[4,256,256]{2,1,0:T(8,128)(2,1)S(1)} %get-tuple-element.24.away, bf16[4,256,256]{2,1,0:T(8,128)(2,1)S(1)} %get-tuple-element.28.home, bf16[2,512,256]{2,1,0:T(8,128)(2,1)S(1)} %get-tuple-element.26.own), custom_call_target="tpu_custom_call" | custom-call | flops 1 | bytes 1 | tf_op jit(solution)/shard_map/diag/pallas_call | solution.py:17
  37.3 3.6 %collective-permute-start.4 = (bf16[4,256,256]{2,1,0:T(8,128)(2,1)S(1)}, bf16[4,256,256]{2,1,0:T(8,128)(2,1)S(1)}, u32[]{:S(2)}, u32[]{:S(2)}) collective-permute-start(bf16[4,256,256]{2,1,0:T(8,128)(2,1)S(1)} %get-tuple-element.28.home), channel_id=1, source_target_pairs={{0,5},{1,508},{2,7},{3,510},{4,9},{5,0},{6,11},{7,2},{8,13},{9,4},... | collective-permute-start | bytes 1572872 | tf_op jit(solution)/shard_map/ppermute | solution.py:210
  40.9 1.9 %collective-permute-start.5 = (f32[2,512,128]{2,1,0:T(8,128)S(1)}, f32[2,512,128]{2,1,0:T(8,128)S(1)}, u32[]{:S(2)}, u32[]{:S(2)}) collective-permute-start(f32[2,512,128]{2,1,0:T(8,128)S(1)} %get-tuple-element.30), channel_id=1, source_target_pairs={{0,1},{1,0},{2,3},{3,2},{4,5},{5,4},{6,7},{7,6},{8,9},{9,8},{10,11... | collective-permute-start | bytes 1572872 | tf_op jit(solution)/shard_map/ppermute | solution.py:210
  42.8 1.9 %mate_middle.1.mate = bf16[2,512,256]{2,1,0:T(8,128)(2,1)S(1)} custom-call(s32[3,1,4]{2,1,0:T(1,128)} %bitcast.8, bf16[2,3,512,512]{3,2,1,0:T(8,128)(2,1)} %copy-done.1, bf16[512,256]{1,0:T(8,128)(2,1)S(1)} %get-tuple-element.23.orbitals), custom_call_target="tpu_custom_call" | custom-call | flops 8000000000 | bytes 1 | tf_op jit(solution)/shard_map/mate_middle/pallas_call | solution.py:17
  44.7 0.0 collective-permute-done.2.same
  44.8 0.8 %collective-permute-done.7.other = bf16[4,256,256]{2,1,0:T(8,128)(2,1)S(1)} collective-permute-done((bf16[4,256,256]{2,1,0:T(8,128)(2,1)S(1)}, bf16[4,256,256]{2,1,0:T(8,128)(2,1)S(1)}, u32[]{:S(2)}, u32[]{:S(2)}) %collective-permute-start.7) | collective-permute-done | bytes 524320 | tf_op jit(solution)/shard_map/ppermute | solution.py:210
  45.6 0.8 %away.1 = (bf16[512,256]{1,0:T(8,128)(2,1)S(1)}, bf16[512,128]{1,0:T(8,128)(2,1)S(1)}) custom-call(bf16[4,256,256]{2,1,0:T(8,128)(2,1)S(1)} %get-tuple-element.24.away, bf16[4,256,256]{2,1,0:T(8,128)(2,1)S(1)} %get-tuple-element.28.home, bf16[2,512,256]{2,1,0:T(8,128)(2,1)S(1)} %collective-permute-done.2.same, ...), custom_call_target="tpu_custom_call" | custom-call | flops 8000000000 | bytes 1 | tf_op jit(solution)/shard_map/away/pallas_call | solution.py:17
  46.3 4.4 %collective-permute-start.8 = (bf16[512,256]{1,0:T(8,128)(2,1)S(1)}, bf16[512,256]{1,0:T(8,128)(2,1)S(1)}, u32[]{:S(2)}, u32[]{:S(2)}) collective-permute-start(bf16[512,256]{1,0:T(8,128)(2,1)S(1)} %get-tuple-element.33), channel_id=1, source_target_pairs={{0,2},{1,3},{2,0},{3,1},{4,6},{5,7},{6,4},{7,5},{8,10},{9,11},{10,... | collective-permute-start | bytes 786440 | tf_op jit(solution)/shard_map/ppermute | solution.py:210
  50.7 2.3 %collective-permute-start.9 = (bf16[512,128]{1,0:T(8,128)(2,1)S(1)}, bf16[512,128]{1,0:T(8,128)(2,1)S(1)}, u32[]{:S(2)}, u32[]{:S(2)}) collective-permute-start(bf16[512,128]{1,0:T(8,128)(2,1)S(1)} %get-tuple-element.34), channel_id=1, source_target_pairs={{0,3},{1,2},{2,1},{3,0},{4,7},{5,6},{6,5},{7,4},{8,11},{9,10},{10,... | collective-permute-start | bytes 393224 | tf_op jit(solution)/shard_map/ppermute | solution.py:210
  53.0 0.8 %home.1 = (f32[2,512,128]{2,1,0:T(8,128)S(1)}, f32[512,128]{1,0:T(8,128)S(1)}) custom-call(bf16[4,256,256]{2,1,0:T(8,128)(2,1)S(1)} %get-tuple-element.24.away, bf16[4,256,256]{2,1,0:T(8,128)(2,1)S(1)} %get-tuple-element.28.home, bf16[2,512,256]{2,1,0:T(8,128)(2,1)S(1)} %collective-permute-done.2.same, bf16[2,512,256]{2,1,0:T(8,128)(2,1)S(1)} %collective-permute-done.3.near, ...), custom_call_target="tpu_custom_call" | custom-call | flops 1 | bytes 1 | tf_op jit(solution)/shard_map/home/pallas_call | solution.py:17
  53.8 2.4 %collective-permute-start.6 = (f32[512,128]{1,0:T(8,128)S(1)}, f32[512,128]{1,0:T(8,128)S(1)}, u32[]{:S(2)}, u32[]{:S(2)}) collective-permute-start(f32[512,128]{1,0:T(8,128)S(1)} %get-tuple-element.31), channel_id=1, source_target_pairs={{0,1},{1,0},{2,3},{3,2},{4,5},{5,4},{6,7},{7,6},{8,9},{9,8},{10,11... | collective-permute-start | bytes 786440 | tf_op jit(solution)/shard_map/ppermute | solution.py:210
  56.3 4.4 %collective-permute-done.9.refs_2_ = bf16[512,128]{1,0:T(8,128)(2,1)S(1)} collective-permute-done((bf16[512,128]{1,0:T(8,128)(2,1)S(1)}, bf16[512,128]{1,0:T(8,128)(2,1)S(1)}, u32[]{:S(2)}, u32[]{:S(2)}) %collective-permute-start.9) | collective-permute-done | bytes 131104 | tf_op jit(solution)/shard_map/ppermute | solution.py:210
  60.7 0.8 %settle.1 = (f32[3,512,128]{2,1,0:T(8,128)}, bf16[512,128]{1,0:T(8,128)(2,1)S(1)}) custom-call(f32[2,512,128]{2,1,0:T(8,128)S(1)} %get-tuple-element.32.refs_0_, bf16[512,256]{1,0:T(8,128)(2,1)S(1)} %collective-permute-done.8.refs_1_, bf16[512,128]{1,0:T(8,128)(2,1)S(1)} %collective-permute-done.9.refs_2_), custom_call_target="tpu_custom_call" | custom-call | flops 8000000000 | bytes 1 | tf_op jit(solution)/shard_map/settle/pallas_call | solution.py:17
  61.6 0.7 %band.1 = f32[3,512,128]{2,1,0:T(8,128)} custom-call(f32[512,128]{1,0:T(8,128)S(1)} %collective-permute-done.6.refs_0_, bf16[512,128]{1,0:T(8,128)(2,1)S(1)} %get-tuple-element.35.refs_1_, f32[3,512,128]{2,1,0:T(8,128)} %get-tuple-element.36.refs_2_), custom_call_target="tpu_custom_call", output_to_operand_aliasing={{}: (2, {})} | custom-call | flops 1 | bytes 1 | tf_op jit(solution)/shard_map/band/pallas_call | solution.py:17
  (8 shorter events, 0.0 us)
Async XLA Ops:
  0.0 2.3 %copy-start = (bf16[2,512,3,512]{3,1,2,0:T(8,128)(2,1)S(1)}, bf16[2,512,3,512]{3,1,2,0:T(8,128)(2,1)}, u32[]{:S(2)}) copy-start(bf16[2,512,3,512]{3,1,2,0:T(8,128)(2,1)} %param.3) | copy-start | bytes 9437188
  2.3 23.8 %collective-permute-start = (bf16[2,3,512,512]{3,2,1,0:T(8,128)(2,1)S(1)}, bf16[2,3,512,512]{3,2,1,0:T(8,128)(2,1)S(1)}, u32[]{:S(2)}, u32[]{:S(2)}) collective-permute-start(bf16[2,3,512,512]{3,2,1,0:T(8,128)(2,1)S(1)} %bitcast.5), channel_id=1, source_target_pairs={{0,1},{1,0},{2,3},{3,2},{4,5},{5,4},{6,7},{7,6},{8,9},{9,8},{10,11... | collective-permute-start | bytes 9437192 | tf_op jit(solution)/shard_map/ppermute | solution.py:210
  11.1 15.0 %collective-permute-start.1 = (bf16[512,256]{1,0:T(8,128)(2,1)S(1)}, bf16[512,256]{1,0:T(8,128)(2,1)S(1)}, u32[]{:S(2)}, u32[]{:S(2)}) collective-permute-start(bf16[512,256]{1,0:T(8,128)(2,1)S(1)} %get-tuple-element.23.orbitals), channel_id=1, source_target_pairs={{0,5},{1,508},{2,7},{3,510},{4,9},{5,0},{6,11},{7,2},{8,13},{9,4},... | collective-permute-start | bytes 786440 | tf_op jit(solution)/shard_map/ppermute | solution.py:210
  20.1 24.6 %collective-permute-start.2 = (bf16[2,512,256]{2,1,0:T(8,128)(2,1)S(1)}, bf16[2,512,256]{2,1,0:T(8,128)(2,1)S(1)}, u32[]{:S(2)}, u32[]{:S(2)}) collective-permute-start(bf16[2,512,256]{2,1,0:T(8,128)(2,1)S(1)} %get-tuple-element.26.own), channel_id=1, source_target_pairs={{0,508},{1,5},{2,510},{3,7},{4,0},{5,9},{6,2},{7,11},{8,4},{9,13},... | collective-permute-start | bytes 1572872 | tf_op jit(solution)/shard_map/ppermute | solution.py:210
  22.0 22.7 %collective-permute-start.3 = (bf16[2,512,256]{2,1,0:T(8,128)(2,1)S(1)}, bf16[2,512,256]{2,1,0:T(8,128)(2,1)S(1)}, u32[]{:S(2)}, u32[]{:S(2)}) collective-permute-start(bf16[2,512,256]{2,1,0:T(8,128)(2,1)S(1)} %get-tuple-element.26.own), channel_id=1, source_target_pairs={{0,5},{1,508},{2,7},{3,510},{4,9},{5,0},{6,11},{7,2},{8,13},{9,4},... | collective-permute-start | bytes 1572872 | tf_op jit(solution)/shard_map/ppermute | solution.py:210
  26.1 1.7 %copy-start.1 = (bf16[2,3,512,512]{3,2,1,0:T(8,128)(2,1)}, bf16[2,3,512,512]{3,2,1,0:T(8,128)(2,1)S(1)}, u32[]{:S(2)}) copy-start(bf16[2,3,512,512]{3,2,1,0:T(8,128)(2,1)S(1)} %collective-permute-done.mate.ints) | copy-start | bytes 9437188
  30.0 15.5 %collective-permute-start.7 = (bf16[4,256,256]{2,1,0:T(8,128)(2,1)S(1)}, bf16[4,256,256]{2,1,0:T(8,128)(2,1)S(1)}, u32[]{:S(2)}, u32[]{:S(2)}) collective-permute-start(bf16[4,256,256]{2,1,0:T(8,128)(2,1)S(1)} %get-tuple-element.24.away), channel_id=1, source_target_pairs={{0,5},{1,508},{2,7},{3,510},{4,9},{5,0},{6,11},{7,2},{8,13},{9,4},... | collective-permute-start | bytes 1572872 | tf_op jit(solution)/shard_map/ppermute | solution.py:210
  37.3 15.8 %collective-permute-start.4 = (bf16[4,256,256]{2,1,0:T(8,128)(2,1)S(1)}, bf16[4,256,256]{2,1,0:T(8,128)(2,1)S(1)}, u32[]{:S(2)}, u32[]{:S(2)}) collective-permute-start(bf16[4,256,256]{2,1,0:T(8,128)(2,1)S(1)} %get-tuple-element.28.home), channel_id=1, source_target_pairs={{0,5},{1,508},{2,7},{3,510},{4,9},{5,0},{6,11},{7,2},{8,13},{9,4},... | collective-permute-start | bytes 1572872 | tf_op jit(solution)/shard_map/ppermute | solution.py:210
  40.9 3.9 %collective-permute-start.5 = (f32[2,512,128]{2,1,0:T(8,128)S(1)}, f32[2,512,128]{2,1,0:T(8,128)S(1)}, u32[]{:S(2)}, u32[]{:S(2)}) collective-permute-start(f32[2,512,128]{2,1,0:T(8,128)S(1)} %get-tuple-element.30), channel_id=1, source_target_pairs={{0,1},{1,0},{2,3},{3,2},{4,5},{5,4},{6,7},{7,6},{8,9},{9,8},{10,11... | collective-permute-start | bytes 1572872 | tf_op jit(solution)/shard_map/ppermute | solution.py:210
  46.3 14.4 %collective-permute-start.8 = (bf16[512,256]{1,0:T(8,128)(2,1)S(1)}, bf16[512,256]{1,0:T(8,128)(2,1)S(1)}, u32[]{:S(2)}, u32[]{:S(2)}) collective-permute-start(bf16[512,256]{1,0:T(8,128)(2,1)S(1)} %get-tuple-element.33), channel_id=1, source_target_pairs={{0,2},{1,3},{2,0},{3,1},{4,6},{5,7},{6,4},{7,5},{8,10},{9,11},{10,... | collective-permute-start | bytes 786440 | tf_op jit(solution)/shard_map/ppermute | solution.py:210
  50.7 10.0 %collective-permute-start.9 = (bf16[512,128]{1,0:T(8,128)(2,1)S(1)}, bf16[512,128]{1,0:T(8,128)(2,1)S(1)}, u32[]{:S(2)}, u32[]{:S(2)}) collective-permute-start(bf16[512,128]{1,0:T(8,128)(2,1)S(1)} %get-tuple-element.34), channel_id=1, source_target_pairs={{0,3},{1,2},{2,1},{3,0},{4,7},{5,6},{6,5},{7,4},{8,11},{9,10},{10,... | collective-permute-start | bytes 393224 | tf_op jit(solution)/shard_map/ppermute | solution.py:210
  53.8 7.7 %collective-permute-start.6 = (f32[512,128]{1,0:T(8,128)S(1)}, f32[512,128]{1,0:T(8,128)S(1)}, u32[]{:S(2)}, u32[]{:S(2)}) collective-permute-start(f32[512,128]{1,0:T(8,128)S(1)} %get-tuple-element.31), channel_id=1, source_target_pairs={{0,1},{1,0},{2,3},{3,2},{4,5},{5,4},{6,7},{7,6},{8,9},{9,8},{10,11... | collective-permute-start | bytes 786440 | tf_op jit(solution)/shard_map/ppermute | solution.py:210

commit v3 on v2

v3 whole, which is shorter than its diff:
```python
import jax
import jax.numpy as jnp
from jax import lax
from jax.experimental import pallas as pl
from jax.experimental.pallas import tpu as pltpu
from jax.sharding import PartitionSpec as P

F32 = jnp.float32
BF16 = jnp.bfloat16
LIMIT = 8 << 20
SMEM = pl.BlockSpec(memory_space=pltpu.SMEM)
VMEM = pl.BlockSpec(memory_space=pltpu.VMEM)
HBM = pl.BlockSpec(memory_space=pltpu.HBM)


def call(kernel, name, specs, outs, operands, scratch=(), cost=1, out_specs=None, aliases=None):
    return pl.pallas_call(
        kernel,
        in_specs=specs,
        out_specs=[VMEM] * len(outs) if out_specs is None else out_specs,
        out_shape=outs,
        scratch_shapes=scratch,
        input_output_aliases=aliases or {},
        compiler_params=pltpu.CompilerParams(vmem_limit_bytes=LIMIT),
        cost_estimate=pl.CostEstimate(flops=int(cost), bytes_accessed=1, transcendentals=0),
        name=name,
    )(*operands)


def in_hbm(value):
    return pltpu.with_memory_space_constraint(value, pltpu.HBM)


def dot_rows(left, right):
    return lax.dot_general(left, right, (((1,), (1,)), ((), ())), preferred_element_type=F32)


def weighted(mask_ref, k, first, plane, orbitals):
    full = jnp.dot(plane[...], orbitals[...], preferred_element_type=F32)
    step = 128
    tiles = [
        full[t * step : (t + 1) * step] * mask_ref[k, 0, first + t].astype(F32)
        for t in range(full.shape[0] // step)
    ]
    return jnp.concatenate(tiles, axis=0).astype(BF16)


def sides():
    aux = lax.axis_index("aux")
    return lax.rem(aux, 2), lax.div(aux, 2)


def own_kernel(mask, ints, orbitals, out, held, edges, mask_ref, planes, sems):
    core, _ = sides()
    per = out.shape[0]
    copies = [
        pltpu.make_async_copy(ints.at[p, 1], planes.at[p], sems.at[p]) for p in range(per)
    ]
    copies.append(pltpu.make_async_copy(orbitals, held, sems.at[per]))
    copies.append(pltpu.make_async_copy(mask, mask_ref, sems.at[per + 1]))
    fetches = [
        pltpu.make_async_copy(ints.at[p, 2 * core], edges.at[p], sems.at[per + 2 + p])
        for p in range(per)
    ]
    for i in (per, 0, per + 1, *range(1, per)):
        copies[i].start()
    for fetch in fetches:
        fetch.start()
    copies[per].wait()
    copies[per + 1].wait()
    for p in range(per):
        copies[p].wait()
        out[p] = weighted(mask_ref, 1, 0, planes.at[p], held)
    for fetch in fetches:
        fetch.wait()


def spot(part, size):
    return pl.ds(pl.multiple_of(part * size, size), size)


def edge_kernel(
    mask, own, mate, orbitals, middle, away, home, bundle, mask_ref, planes, sems
):
    core, far = sides()
    side = 2 - 2 * core
    per, rows, _ = planes.shape
    mid = rows // 2
    copies = [
        pltpu.make_async_copy(own.at[p, side], planes.at[p], sems.at[p]) for p in range(per)
    ]
    copies.append(pltpu.make_async_copy(mask, mask_ref, sems.at[per]))
    for copy in copies:
        copy.start()
    copies[per].wait()
    for p in (*range(per, 2 * per), *range(per)):
        if p < per:
            copies[p].wait()
        source = planes.at[p] if p < per else mate.at[p - per]
        for out, part in ((away, 1 - far), (home, far)):
            plane = source.at[spot(part, mid)]
            half = weighted(mask_ref, side, 2 * part, plane, orbitals)
            out[p] = half
            bundle[p, spot(part, mid), :] = half
    for p in range(per):
        bundle[2 * per + p] = middle[p]


def product(left, right):
    total = dot_rows(left[0][...], right[0][...])
    for i in range(1, len(left)):
        total += dot_rows(left[i][...], right[i][...])
    return total


def planes_of(ref, count, rows):
    return [ref.at[p, rows] for p in range(count)]


def diag_kernel(mine, theirs, out):
    core, _ = sides()
    count, rows, _ = mine.shape
    quarter = out.shape[2]
    spots = [spot(2 * h + core, quarter) for h in range(2)]
    band = rows // 2
    for r in range(2):
        lines = pl.ds(r * band, band)
        total = None
        for ref in (mine, theirs):
            for p in range(count):
                right = jnp.concatenate([ref[p, where, :] for where in spots], axis=0)
                term = dot_rows(ref[p, lines, :], right)
                total = term if total is None else total + term
        for h in range(2):
            out[h, lines, :] = total[:, h * quarter : (h + 1) * quarter]


def shared_kernel(away, home, same, near, out):
    _, far = sides()
    count, mid, _ = away.shape
    per = same.shape[0]
    cols = spot(1 - far, mid)
    rights = planes_of(same, per, cols) + planes_of(near, per, cols)
    for band, left in ((1 - far, away), (far, home)):
        out[spot(band, mid), :] = product(planes_of(left, count, pl.ds(0, mid)), rights)


def middle_part(rows, own, mate, other):
    per = own.shape[0]
    rights = [other.at[per + p] for p in range(per)] + [other.at[p] for p in range(per)]
    mates = [mate.at[2 * per + p, rows] for p in range(per)]
    return product(planes_of(own, per, rows) + mates, rights)


def away_kernel(part, own, mate, other, diag, straight, crossed):
    core, far = sides()
    width = crossed.shape[1]
    mid = 2 * width
    for r in range(2):
        rows = pl.ds(r * mid, mid)
        total = part[rows, :] + middle_part(rows, own, mate, other)
        first, second = total[:, :width], total[:, width:]
        straight[rows, :width] = jnp.where(core == 0, first, second).astype(BF16)
        crossed[rows, :] = jnp.where(core == 0, second, first).astype(BF16)
        straight[rows, width:] = diag[1 - far, rows, :].astype(BF16)


def home_kernel(away, home, same, near, own, mate, other, diag, held, sent):
    core, far = sides()
    count, mid, _ = away.shape
    per = own.shape[0]
    width = sent.shape[1]
    cols = spot(far, mid)
    rights = planes_of(same, per, cols) + planes_of(near, per, cols)
    for band, left in ((1 - far, away), (far, home)):
        rows = spot(band, mid)
        total = product(planes_of(left, count, pl.ds(0, mid)), rights)
        total += middle_part(rows, own, mate, other)
        first, second = total[:, :width], total[:, width:]
        held[0, rows, :] = jnp.where(core == 0, first, second)
        held[1, rows, :] = diag[far, rows, :]
        sent[rows, :] = jnp.where(core == 0, second, first)


def settle_kernel(scale, kept, straight, crossed, out, cross, held, sems):
    core, _ = sides()
    width = crossed.shape[1]
    copies = []
    for i, place in enumerate((2 - 2 * core, 1)):
        held[i] = (kept[i] + straight[:, i * width : (i + 1) * width].astype(F32)) * scale
        copies.append(pltpu.make_async_copy(held.at[i], out.at[place], sems.at[i]))
        copies[i].start()
    cross[...] = crossed[...]
    for copy in copies:
        copy.wait()


def band_kernel(scale, got, cross, band, out, held, sems):
    core, _ = sides()
    held[...] = (got[...] + cross[...].astype(F32)) * scale
    copy = pltpu.make_async_copy(held, out.at[2 * core], sems.at[0])
    copy.start()
    copy.wait()


def body(ints3c, coef, tile_mask):
    blocks = lax.axis_size("blk")
    group = lax.axis_size("aux")
    mask = jnp.transpose(tile_mask, (1, 0, 2))
    ints = jnp.transpose(ints3c, (0, 2, 1, 3))
    mask, coef, ints = in_hbm(mask), in_hbm(coef), in_hbm(ints)
    per, _, rows, inner = ints.shape
    cols = coef.shape[1]
    mid, quarter = rows // 2, rows // group

    def device(b, a):
        return (b % blocks) * group + a

    members = [(b, a) for b in range(blocks) for a in range(group)]

    def moved(value, target):
        pairs = [(device(b, a), target(b, a)) for b, a in members]
        return lax.ppermute(value, ("blk", "aux"), pairs)

    def to_edge(value):
        return moved(value, lambda b, a: device(b + 1 - 2 * (a % 2), a ^ 1))

    def to_same(value):
        return moved(value, lambda b, a: device(b - 1 + 2 * (a % 2), a))

    def within(value, flip):
        return moved(value, lambda b, a: device(b, a ^ flip))

    half = jax.ShapeDtypeStruct((per, rows, cols), BF16)
    smem = pltpu.SMEM(mask.shape, mask.dtype)
    planes = pltpu.VMEM((per, rows, inner), BF16)
    own_half, coef, edges = call(
        own_kernel,
        "own_middle",
        [HBM, HBM, HBM],
        [
            half,
            jax.ShapeDtypeStruct(coef.shape, BF16),
            jax.ShapeDtypeStruct((per, rows, inner), BF16),
        ],
        (mask, ints, coef),
        [smem, planes, pltpu.SemaphoreType.DMA((2 * per + 2,))],
    )
    ints, own_half = lax.optimization_barrier((ints, own_half))
    ints = in_hbm(ints)
    edge_coef = to_edge(coef)
    mate_edges = within(edges, 1)
    same = to_same(own_half)
    near = to_edge(own_half)
    part = jax.ShapeDtypeStruct((2 * per, mid, cols), BF16)
    away, home, bundle = call(
        edge_kernel,
        "edge_half",
        [HBM, HBM, VMEM, VMEM, VMEM],
        [part, part, jax.ShapeDtypeStruct((3 * per, rows, cols), BF16)],
        (mask, ints, mate_edges, edge_coef, own_half),
        [
            smem,
            planes,
            pltpu.SemaphoreType.DMA((per + 1,)),
        ],
        cost=COSTS["edge"],
    )
    other_away = to_edge(away)
    pair = jax.ShapeDtypeStruct((2, rows, quarter), F32)
    mate_bundle = within(bundle, 1)
    other_home = to_edge(home)
    (diag,) = call(
        diag_kernel, "diag", [VMEM, VMEM], [pair], (bundle, mate_bundle), cost=COSTS["diag"]
    )

    (first_part,) = call(
        shared_kernel,
        "shared",
        [VMEM] * 4,
        [jax.ShapeDtypeStruct((rows, mid), F32)],
        (away, home, same, near),
        cost=COSTS["shared"],
    )
    quarters = jax.ShapeDtypeStruct((rows, quarter), BF16)
    straight, crossed = call(
        away_kernel,
        "away",
        [VMEM] * 5,
        [jax.ShapeDtypeStruct((rows, mid), BF16), quarters],
        (first_part, own_half, mate_bundle, other_away, diag),
        cost=COSTS["away"],
    )
    straight = within(straight, 2)
    crossed = within(crossed, 3)
    held, sent = call(
        home_kernel,
        "home",
        [VMEM] * 8,
        [pair, jax.ShapeDtypeStruct((rows, quarter), F32)],
        (away, home, same, near, own_half, mate_bundle, other_home, diag),
        cost=COSTS["home"],
    )
    got = within(sent, 1)
    scale = (group * per * 3 * cols) ** (-0.5)
    whole = jax.ShapeDtypeStruct((3, rows, quarter), F32)
    band, cross = call(
        lambda *refs: settle_kernel(scale, *refs),
        "settle",
        [VMEM] * 3,
        [whole, quarters],
        (held, straight, crossed),
        [pltpu.VMEM((2, rows, quarter), F32), pltpu.SemaphoreType.DMA((2,))],
        out_specs=[HBM, VMEM],
        cost=COSTS["settle"],
    )
    (band,) = call(
        lambda *refs: band_kernel(scale, *refs),
        "band",
        [VMEM, VMEM, HBM],
        [whole],
        (got, cross, band),
        [pltpu.VMEM((rows, quarter), F32), pltpu.SemaphoreType.DMA((1,))],
        out_specs=[HBM],
        aliases={2: 0},
    )
    return jnp.transpose(band, (1, 0, 2))


COSTS = {"edge": 3e9, "diag": 1, "shared": 2e10, "away": 8e9, "home": 1, "settle": 8e9}


def solution(mesh):
    placed = (P("aux", "blk", None, None), P("blk", None), P("blk", None, None))
    return jax.shard_map(
        body, mesh=mesh, in_specs=placed, out_specs=P("blk", None, "aux"), check_vma=False
    )
```

time: 62.7 us -> 61.3 us (0.978)
  the two profiles are of different devices: /device:TPU:1 before, /device:TPU:3 now
where the time goes in v3:
time: 61.3 us; the launch traced here: 60.9 us
  starting transfers between devices  32.2 us (53%)
  waiting for transfers between devices  20.2 us (33%)
  Pallas kernels  8.33 us (14%)
    ppermute x10, starting transfers between devices, moved(): return lax.ppermute(value, ('blk', 'aux'), pairs)  32.2 us
    ppermute x10, waiting for transfers between devices, moved(): return lax.ppermute(value, ('blk', 'aux'), pairs)  20.2 us
    pallas_call x8, Pallas kernels, call(): pl.pallas_call(kernel, in_specs=specs, out_specs=[VMEM] * len(outs) if ou...  8.33 us
  transfers between devices with their start and end apart: 10, of which 2 were waited for; matrix products, arithmetic and copies ran while one was open for 0% of the time, Pallas kernels for 9%

profile of v3, /device:TPU:3, one launch (start us, length us, event | category | flops | bytes accessed | tf_op | source)
XLA Modules:
  0.0 60.9 jit_solution(5580793811893883341)
XLA Ops:
  0.0 2.0 %own_middle.1 = (bf16[2,512,256]{2,1,0:T(8,128)(2,1)S(1)}, bf16[512,256]{1,0:T(8,128)(2,1)S(1)}, bf16[2,512,512]{2,1,0:T(8,128)(2,1)S(1)}) custom-call(s32[3,1,4]{2,1,0:T(1,128)} %bitcast.5, bf16[2,3,512,512]{3,2,1,0:T(8,128)(2,1)} %bitcast.3, bf16[512,256]{1,0:T(8,128)(2,1)} %orbitals.1), custom_call_target="tpu_custom_call" | custom-call | flops 1 | bytes 1 | tf_op jit(solution)/shard_map/own_middle/pallas_call | solution.py:17
  2.0 2.6 %collective-permute-start = (bf16[2,512,512]{2,1,0:T(8,128)(2,1)S(1)}, bf16[2,512,512]{2,1,0:T(8,128)(2,1)S(1)}, u32[]{:S(2)}, u32[]{:S(2)}) collective-permute-start(bf16[2,512,512]{2,1,0:T(8,128)(2,1)S(1)} %get-tuple-element.21), channel_id=1, source_target_pairs={{0,1},{1,0},{2,3},{3,2},{4,5},{5,4},{6,7},{7,6},{8,9},{9,8},{10,11... | collective-permute-start | bytes 3145736 | tf_op jit(solution)/shard_map/ppermute | solution.py:223
  4.6 5.0 %collective-permute-start.1 = (bf16[512,256]{1,0:T(8,128)(2,1)S(1)}, bf16[512,256]{1,0:T(8,128)(2,1)S(1)}, u32[]{:S(2)}, u32[]{:S(2)}) collective-permute-start(bf16[512,256]{1,0:T(8,128)(2,1)S(1)} %get-tuple-element.22), channel_id=1, source_target_pairs={{0,5},{1,508},{2,7},{3,510},{4,9},{5,0},{6,11},{7,2},{8,13},{9,4},... | collective-permute-start | bytes 786440 | tf_op jit(solution)/shard_map/ppermute | solution.py:223
  9.6 1.9 %collective-permute-start.2 = (bf16[2,512,256]{2,1,0:T(8,128)(2,1)S(1)}, bf16[2,512,256]{2,1,0:T(8,128)(2,1)S(1)}, u32[]{:S(2)}, u32[]{:S(2)}) collective-permute-start(bf16[2,512,256]{2,1,0:T(8,128)(2,1)S(1)} %get-tuple-element.23.middle.own), channel_id=1, source_target_pairs={{0,508},{1,5},{2,510},{3,7},{4,0},{5,9},{6,2},{7,11},{8,4},{9,13},... | collective-permute-start | bytes 1572872 | tf_op jit(solution)/shard_map/ppermute | solution.py:223
  11.5 4.0 %collective-permute-start.3 = (bf16[2,512,256]{2,1,0:T(8,128)(2,1)S(1)}, bf16[2,512,256]{2,1,0:T(8,128)(2,1)S(1)}, u32[]{:S(2)}, u32[]{:S(2)}) collective-permute-start(bf16[2,512,256]{2,1,0:T(8,128)(2,1)S(1)} %get-tuple-element.23.middle.own), channel_id=1, source_target_pairs={{0,5},{1,508},{2,7},{3,510},{4,9},{5,0},{6,11},{7,2},{8,13},{9,4},... | collective-permute-start | bytes 1572872 | tf_op jit(solution)/shard_map/ppermute | solution.py:223
  15.6 0.0 collective-permute-done.1.orbitals
  15.6 2.0 %edge_half.1 = (bf16[4,256,256]{2,1,0:T(8,128)(2,1)S(1)}, bf16[4,256,256]{2,1,0:T(8,128)(2,1)S(1)}, bf16[6,512,256]{2,1,0:T(8,128)(2,1)S(1)}) custom-call(s32[3,1,4]{2,1,0:T(1,128)} %bitcast.6, bf16[2,3,512,512]{3,2,1,0:T(8,128)(2,1)} %bitcast.4, bf16[2,512,512]{2,1,0:T(8,128)(2,1)S(1)} %collective-permute-done.mate, ...), custom_call_target="tpu_custom_call" | custom-call | flops 3000000000 | bytes 1 | tf_op jit(solution)/shard_map/edge_half/pallas_call | solution.py:17
  17.6 1.9 %collective-permute-start.4 = (bf16[6,512,256]{2,1,0:T(8,128)(2,1)S(1)}, bf16[6,512,256]{2,1,0:T(8,128)(2,1)S(1)}, u32[]{:S(2)}, u32[]{:S(2)}) collective-permute-start(bf16[6,512,256]{2,1,0:T(8,128)(2,1)S(1)} %get-tuple-element.26.mine), channel_id=1, source_target_pairs={{0,1},{1,0},{2,3},{3,2},{4,5},{5,4},{6,7},{7,6},{8,9},{9,8},{10,11... | collective-permute-start | bytes 4718600 | tf_op jit(solution)/shard_map/ppermute | solution.py:223
  19.5 3.8 %collective-permute-start.7 = (bf16[4,256,256]{2,1,0:T(8,128)(2,1)S(1)}, bf16[4,256,256]{2,1,0:T(8,128)(2,1)S(1)}, u32[]{:S(2)}, u32[]{:S(2)}) collective-permute-start(bf16[4,256,256]{2,1,0:T(8,128)(2,1)S(1)} %get-tuple-element.24.away), channel_id=1, source_target_pairs={{0,5},{1,508},{2,7},{3,510},{4,9},{5,0},{6,11},{7,2},{8,13},{9,4},... | collective-permute-start | bytes 1572872 | tf_op jit(solution)/shard_map/ppermute | solution.py:223
  23.3 3.9 %collective-permute-start.5 = (bf16[4,256,256]{2,1,0:T(8,128)(2,1)S(1)}, bf16[4,256,256]{2,1,0:T(8,128)(2,1)S(1)}, u32[]{:S(2)}, u32[]{:S(2)}) collective-permute-start(bf16[4,256,256]{2,1,0:T(8,128)(2,1)S(1)} %get-tuple-element.25.home), channel_id=1, source_target_pairs={{0,5},{1,508},{2,7},{3,510},{4,9},{5,0},{6,11},{7,2},{8,13},{9,4},... | collective-permute-start | bytes 1572872 | tf_op jit(solution)/shard_map/ppermute | solution.py:223
  27.2 0.0 collective-permute-done.2.same
  27.2 0.0 collective-permute-done.3.near
  27.2 0.5 shared.1.part
  27.7 0.0 collective-permute-done.4.theirs.mate
  27.7 1.0 %diag.1 = f32[2,512,128]{2,1,0:T(8,128)S(1)} custom-call(bf16[6,512,256]{2,1,0:T(8,128)(2,1)S(1)} %get-tuple-element.26.mine, bf16[6,512,256]{2,1,0:T(8,128)(2,1)S(1)} %collective-permute-done.4.theirs.mate), custom_call_target="tpu_custom_call" | custom-call | flops 1 | bytes 1 | tf_op jit(solution)/shard_map/diag/pallas_call | solution.py:17
  28.8 4.1 %collective-permute-done.7.other = bf16[4,256,256]{2,1,0:T(8,128)(2,1)S(1)} collective-permute-done((bf16[4,256,256]{2,1,0:T(8,128)(2,1)S(1)}, bf16[4,256,256]{2,1,0:T(8,128)(2,1)S(1)}, u32[]{:S(2)}, u32[]{:S(2)}) %collective-permute-start.7) | collective-permute-done | bytes 524320 | tf_op jit(solution)/shard_map/ppermute | solution.py:223
  32.9 0.5 away.1
  33.3 4.0 %collective-permute-start.8 = (bf16[512,256]{1,0:T(8,128)(2,1)S(1)}, bf16[512,256]{1,0:T(8,128)(2,1)S(1)}, u32[]{:S(2)}, u32[]{:S(2)}) collective-permute-start(bf16[512,256]{1,0:T(8,128)(2,1)S(1)} %get-tuple-element.29), channel_id=1, source_target_pairs={{0,2},{1,3},{2,0},{3,1},{4,6},{5,7},{6,4},{7,5},{8,10},{9,11},{10,... | collective-permute-start | bytes 786440 | tf_op jit(solution)/shard_map/ppermute | solution.py:223
  37.4 1.9 %collective-permute-start.9 = (bf16[512,128]{1,0:T(8,128)(2,1)S(1)}, bf16[512,128]{1,0:T(8,128)(2,1)S(1)}, u32[]{:S(2)}, u32[]{:S(2)}) collective-permute-start(bf16[512,128]{1,0:T(8,128)(2,1)S(1)} %get-tuple-element.30), channel_id=1, source_target_pairs={{0,3},{1,2},{2,1},{3,0},{4,7},{5,6},{6,5},{7,4},{8,11},{9,10},{10,... | collective-permute-start | bytes 393224 | tf_op jit(solution)/shard_map/ppermute | solution.py:223
  39.3 0.8 %home.1 = (f32[2,512,128]{2,1,0:T(8,128)S(1)}, f32[512,128]{1,0:T(8,128)S(1)}) custom-call(bf16[4,256,256]{2,1,0:T(8,128)(2,1)S(1)} %get-tuple-element.24.away, bf16[4,256,256]{2,1,0:T(8,128)(2,1)S(1)} %get-tuple-element.25.home, bf16[2,512,256]{2,1,0:T(8,128)(2,1)S(1)} %collective-permute-done.2.same, bf16[2,512,256]{2,1,0:T(8,128)(2,1)S(1)} %collective-permute-done.3.near, ...), custom_call_target="tpu_custom_call" | custom-call | flops 1 | bytes 1 | tf_op jit(solution)/shard_map/home/pallas_call | solution.py:17
  40.1 3.1 %collective-permute-start.6 = (f32[512,128]{1,0:T(8,128)S(1)}, f32[512,128]{1,0:T(8,128)S(1)}, u32[]{:S(2)}, u32[]{:S(2)}) collective-permute-start(f32[512,128]{1,0:T(8,128)S(1)} %get-tuple-element.27), channel_id=1, source_target_pairs={{0,1},{1,0},{2,3},{3,2},{4,5},{5,4},{6,7},{7,6},{8,9},{9,8},{10,11... | collective-permute-start | bytes 786440 | tf_op jit(solution)/shard_map/ppermute | solution.py:223
  43.3 16.0 %collective-permute-done.9.refs_2_ = bf16[512,128]{1,0:T(8,128)(2,1)S(1)} collective-permute-done((bf16[512,128]{1,0:T(8,128)(2,1)S(1)}, bf16[512,128]{1,0:T(8,128)(2,1)S(1)}, u32[]{:S(2)}, u32[]{:S(2)}) %collective-permute-start.9) | collective-permute-done | bytes 131104 | tf_op jit(solution)/shard_map/ppermute | solution.py:223
  59.3 0.8 %settle.1 = (f32[3,512,128]{2,1,0:T(8,128)}, bf16[512,128]{1,0:T(8,128)(2,1)S(1)}) custom-call(f32[2,512,128]{2,1,0:T(8,128)S(1)} %get-tuple-element.28.refs_0_, bf16[512,256]{1,0:T(8,128)(2,1)S(1)} %collective-permute-done.8.refs_1_, bf16[512,128]{1,0:T(8,128)(2,1)S(1)} %collective-permute-done.9.refs_2_), custom_call_target="tpu_custom_call" | custom-call | flops 8000000000 | bytes 1 | tf_op jit(solution)/shard_map/settle/pallas_call | solution.py:17
  60.1 0.7 %band.1 = f32[3,512,128]{2,1,0:T(8,128)} custom-call(f32[512,128]{1,0:T(8,128)S(1)} %collective-permute-done.6.refs_0_, bf16[512,128]{1,0:T(8,128)(2,1)S(1)} %get-tuple-element.31.refs_1_, f32[3,512,128]{2,1,0:T(8,128)} %get-tuple-element.32.refs_2_), custom_call_target="tpu_custom_call", output_to_operand_aliasing={{}: (2, {})} | custom-call | flops 1 | bytes 1 | tf_op jit(solution)/shard_map/band/pallas_call | solution.py:17
  (4 shorter events, 0.0 us)
Async XLA Ops:
  2.0 13.5 %collective-permute-start = (bf16[2,512,512]{2,1,0:T(8,128)(2,1)S(1)}, bf16[2,512,512]{2,1,0:T(8,128)(2,1)S(1)}, u32[]{:S(2)}, u32[]{:S(2)}) collective-permute-start(bf16[2,512,512]{2,1,0:T(8,128)(2,1)S(1)} %get-tuple-element.21), channel_id=1, source_target_pairs={{0,1},{1,0},{2,3},{3,2},{4,5},{5,4},{6,7},{7,6},{8,9},{9,8},{10,11... | collective-permute-start | bytes 3145736 | tf_op jit(solution)/shard_map/ppermute | solution.py:223
  4.6 10.9 %collective-permute-start.1 = (bf16[512,256]{1,0:T(8,128)(2,1)S(1)}, bf16[512,256]{1,0:T(8,128)(2,1)S(1)}, u32[]{:S(2)}, u32[]{:S(2)}) collective-permute-start(bf16[512,256]{1,0:T(8,128)(2,1)S(1)} %get-tuple-element.22), channel_id=1, source_target_pairs={{0,5},{1,508},{2,7},{3,510},{4,9},{5,0},{6,11},{7,2},{8,13},{9,4},... | collective-permute-start | bytes 786440 | tf_op jit(solution)/shard_map/ppermute | solution.py:223
  9.6 17.6 %collective-permute-start.2 = (bf16[2,512,256]{2,1,0:T(8,128)(2,1)S(1)}, bf16[2,512,256]{2,1,0:T(8,128)(2,1)S(1)}, u32[]{:S(2)}, u32[]{:S(2)}) collective-permute-start(bf16[2,512,256]{2,1,0:T(8,128)(2,1)S(1)} %get-tuple-element.23.middle.own), channel_id=1, source_target_pairs={{0,508},{1,5},{2,510},{3,7},{4,0},{5,9},{6,2},{7,11},{8,4},{9,13},... | collective-permute-start | bytes 1572872 | tf_op jit(solution)/shard_map/ppermute | solution.py:223
  11.5 15.7 %collective-permute-start.3 = (bf16[2,512,256]{2,1,0:T(8,128)(2,1)S(1)}, bf16[2,512,256]{2,1,0:T(8,128)(2,1)S(1)}, u32[]{:S(2)}, u32[]{:S(2)}) collective-permute-start(bf16[2,512,256]{2,1,0:T(8,128)(2,1)S(1)} %get-tuple-element.23.middle.own), channel_id=1, source_target_pairs={{0,5},{1,508},{2,7},{3,510},{4,9},{5,0},{6,11},{7,2},{8,13},{9,4},... | collective-permute-start | bytes 1572872 | tf_op jit(solution)/shard_map/ppermute | solution.py:223
  17.6 10.2 %collective-permute-start.4 = (bf16[6,512,256]{2,1,0:T(8,128)(2,1)S(1)}, bf16[6,512,256]{2,1,0:T(8,128)(2,1)S(1)}, u32[]{:S(2)}, u32[]{:S(2)}) collective-permute-start(bf16[6,512,256]{2,1,0:T(8,128)(2,1)S(1)} %get-tuple-element.26.mine), channel_id=1, source_target_pairs={{0,1},{1,0},{2,3},{3,2},{4,5},{5,4},{6,7},{7,6},{8,9},{9,8},{10,11... | collective-permute-start | bytes 4718600 | tf_op jit(solution)/shard_map/ppermute | solution.py:223
  19.5 13.4 %collective-permute-start.7 = (bf16[4,256,256]{2,1,0:T(8,128)(2,1)S(1)}, bf16[4,256,256]{2,1,0:T(8,128)(2,1)S(1)}, u32[]{:S(2)}, u32[]{:S(2)}) collective-permute-start(bf16[4,256,256]{2,1,0:T(8,128)(2,1)S(1)} %get-tuple-element.24.away), channel_id=1, source_target_pairs={{0,5},{1,508},{2,7},{3,510},{4,9},{5,0},{6,11},{7,2},{8,13},{9,4},... | collective-permute-start | bytes 1572872 | tf_op jit(solution)/shard_map/ppermute | solution.py:223
  23.3 16.0 %collective-permute-start.5 = (bf16[4,256,256]{2,1,0:T(8,128)(2,1)S(1)}, bf16[4,256,256]{2,1,0:T(8,128)(2,1)S(1)}, u32[]{:S(2)}, u32[]{:S(2)}) collective-permute-start(bf16[4,256,256]{2,1,0:T(8,128)(2,1)S(1)} %get-tuple-element.25.home), channel_id=1, source_target_pairs={{0,5},{1,508},{2,7},{3,510},{4,9},{5,0},{6,11},{7,2},{8,13},{9,4},... | collective-permute-start | bytes 1572872 | tf_op jit(solution)/shard_map/ppermute | solution.py:223
  33.3 25.9 %collective-permute-start.8 = (bf16[512,256]{1,0:T(8,128)(2,1)S(1)}, bf16[512,256]{1,0:T(8,128)(2,1)S(1)}, u32[]{:S(2)}, u32[]{:S(2)}) collective-permute-start(bf16[512,256]{1,0:T(8,128)(2,1)S(1)} %get-tuple-element.29), channel_id=1, source_target_pairs={{0,2},{1,3},{2,0},{3,1},{4,6},{5,7},{6,4},{7,5},{8,10},{9,11},{10,... | collective-permute-start | bytes 786440 | tf_op jit(solution)/shard_map/ppermute | solution.py:223
  37.4 21.9 %collective-permute-start.9 = (bf16[512,128]{1,0:T(8,128)(2,1)S(1)}, bf16[512,128]{1,0:T(8,128)(2,1)S(1)}, u32[]{:S(2)}, u32[]{:S(2)}) collective-permute-start(bf16[512,128]{1,0:T(8,128)(2,1)S(1)} %get-tuple-element.30), channel_id=1, source_target_pairs={{0,3},{1,2},{2,1},{3,0},{4,7},{5,6},{6,5},{7,4},{8,11},{9,10},{10,... | collective-permute-start | bytes 393224 | tf_op jit(solution)/shard_map/ppermute | solution.py:223
  40.1 20.0 %collective-permute-start.6 = (f32[512,128]{1,0:T(8,128)S(1)}, f32[512,128]{1,0:T(8,128)S(1)}, u32[]{:S(2)}, u32[]{:S(2)}) collective-permute-start(f32[512,128]{1,0:T(8,128)S(1)} %get-tuple-element.27), channel_id=1, source_target_pairs={{0,1},{1,0},{2,3},{3,2},{4,5},{5,4},{6,7},{7,6},{8,9},{9,8},{10,11... | collective-permute-start | bytes 786440 | tf_op jit(solution)/shard_map/ppermute | solution.py:223

commit v4 on v3

--- a/solution.py
+++ b/solution.py
@@ -182,25 +182,28 @@
         sent[rows, :] = jnp.where(core == 0, second, first)
 
 
-def settle_kernel(scale, kept, straight, crossed, out, cross, held, sems):
+def settle_kernel(scale, kept, straight, crossed, held, cross):
+    width = crossed.shape[1]
+    for i in range(2):
+        part = straight[:, i * width : (i + 1) * width].astype(F32)
+        held[i] = (kept[i] + part) * scale
+    cross[...] = crossed[...]
+
+
+def band_kernel(scale, got, cross, done, out, held, sems):
     core, _ = sides()
-    width = crossed.shape[1]
-    copies = []
-    for i, place in enumerate((2 - 2 * core, 1)):
-        held[i] = (kept[i] + straight[:, i * width : (i + 1) * width].astype(F32)) * scale
-        copies.append(pltpu.make_async_copy(held.at[i], out.at[place], sems.at[i]))
-        copies[i].start()
-    cross[...] = crossed[...]
+    copies = [
+        pltpu.make_async_copy(source, out.at[place], sems.at[i])
+        for i, (source, place) in enumerate(
+            ((done.at[0], 2 - 2 * core), (done.at[1], 1), (held, 2 * core))
+        )
+    ]
+    copies[0].start()
+    copies[1].start()
+    held[...] = (got[...] + cross[...].astype(F32)) * scale
+    copies[2].start()
     for copy in copies:
         copy.wait()
-
-
-def band_kernel(scale, got, cross, band, out, held, sems):
-    core, _ = sides()
-    held[...] = (got[...] + cross[...].astype(F32)) * scale
-    copy = pltpu.make_async_copy(held, out.at[2 * core], sems.at[0])
-    copy.start()
-    copy.wait()
 
 
 def body(ints3c, coef, tile_mask):
@@ -304,25 +307,22 @@
     got = within(sent, 1)
     scale = (group * per * 3 * cols) ** (-0.5)
     whole = jax.ShapeDtypeStruct((3, rows, quarter), F32)
-    band, cross = call(
+    done, cross = call(
         lambda *refs: settle_kernel(scale, *refs),
         "settle",
         [VMEM] * 3,
-        [whole, quarters],
+        [pair, quarters],
         (held, straight, crossed),
-        [pltpu.VMEM((2, rows, quarter), F32), pltpu.SemaphoreType.DMA((2,))],
-        out_specs=[HBM, VMEM],
         cost=COSTS["settle"],
     )
     (band,) = call(
         lambda *refs: band_kernel(scale, *refs),
         "band",
-        [VMEM, VMEM, HBM],
+        [VMEM] * 3,
         [whole],
-        (got, cross, band),
-        [pltpu.VMEM((rows, quarter), F32), pltpu.SemaphoreType.DMA((1,))],
+        (got, cross, done),
+        [pltpu.VMEM((rows, quarter), F32), pltpu.SemaphoreType.DMA((3,))],
         out_specs=[HBM],
-        aliases={2: 0},
     )
     return jnp.transpose(band, (1, 0, 2))
 

time: 61.3 us -> 60.7 us (level)
  transfers between devices with their start and end apart: 10 -> 10, of which waited for: 2 -> 2; matrix products, arithmetic and copies ran while one was open for 0% -> 0% of each run, Pallas kernels for 9% -> 8%
where the time goes in v4:
time: 60.7 us; the launch traced here: 60.3 us
  starting transfers between devices  32.2 us (53%)
  waiting for transfers between devices  20.2 us (33%)
  Pallas kernels  7.73 us (13%)
    ppermute x10, starting transfers between devices, moved(): return lax.ppermute(value, ('blk', 'aux'), pairs)  32.2 us
    ppermute x10, waiting for transfers between devices, moved(): return lax.ppermute(value, ('blk', 'aux'), pairs)  20.2 us
    pallas_call x8, Pallas kernels, call(): pl.pallas_call(kernel, in_specs=specs, out_specs=[VMEM] * len(outs) if ou...  7.73 us
  transfers between devices with their start and end apart: 10, of which 2 were waited for; matrix products, arithmetic and copies ran while one was open for 0% of the time, Pallas kernels for 8%

profile of v4, /device:TPU:3, one launch (start us, length us, event | category | flops | bytes accessed | tf_op | source)
XLA Modules:
  0.0 60.3 jit_solution(10289726687150293596)
XLA Ops:
  0.0 2.0 %own_middle.1 = (bf16[2,512,256]{2,1,0:T(8,128)(2,1)S(1)}, bf16[512,256]{1,0:T(8,128)(2,1)S(1)}, bf16[2,512,512]{2,1,0:T(8,128)(2,1)S(1)}) custom-call(s32[3,1,4]{2,1,0:T(1,128)} %bitcast.5, bf16[2,3,512,512]{3,2,1,0:T(8,128)(2,1)} %bitcast.3, bf16[512,256]{1,0:T(8,128)(2,1)} %orbitals.1), custom_call_target="tpu_custom_call" | custom-call | flops 1 | bytes 1 | tf_op jit(solution)/shard_map/own_middle/pallas_call | solution.py:17
  2.0 2.6 %collective-permute-start = (bf16[2,512,512]{2,1,0:T(8,128)(2,1)S(1)}, bf16[2,512,512]{2,1,0:T(8,128)(2,1)S(1)}, u32[]{:S(2)}, u32[]{:S(2)}) collective-permute-start(bf16[2,512,512]{2,1,0:T(8,128)(2,1)S(1)} %get-tuple-element.21), channel_id=1, source_target_pairs={{0,1},{1,0},{2,3},{3,2},{4,5},{5,4},{6,7},{7,6},{8,9},{9,8},{10,11... | collective-permute-start | bytes 3145736 | tf_op jit(solution)/shard_map/ppermute | solution.py:226
  4.6 5.0 %collective-permute-start.1 = (bf16[512,256]{1,0:T(8,128)(2,1)S(1)}, bf16[512,256]{1,0:T(8,128)(2,1)S(1)}, u32[]{:S(2)}, u32[]{:S(2)}) collective-permute-start(bf16[512,256]{1,0:T(8,128)(2,1)S(1)} %get-tuple-element.22), channel_id=1, source_target_pairs={{0,5},{1,508},{2,7},{3,510},{4,9},{5,0},{6,11},{7,2},{8,13},{9,4},... | collective-permute-start | bytes 786440 | tf_op jit(solution)/shard_map/ppermute | solution.py:226
  9.6 1.9 %collective-permute-start.2 = (bf16[2,512,256]{2,1,0:T(8,128)(2,1)S(1)}, bf16[2,512,256]{2,1,0:T(8,128)(2,1)S(1)}, u32[]{:S(2)}, u32[]{:S(2)}) collective-permute-start(bf16[2,512,256]{2,1,0:T(8,128)(2,1)S(1)} %get-tuple-element.23.middle.own), channel_id=1, source_target_pairs={{0,508},{1,5},{2,510},{3,7},{4,0},{5,9},{6,2},{7,11},{8,4},{9,13},... | collective-permute-start | bytes 1572872 | tf_op jit(solution)/shard_map/ppermute | solution.py:226
  11.5 4.0 %collective-permute-start.3 = (bf16[2,512,256]{2,1,0:T(8,128)(2,1)S(1)}, bf16[2,512,256]{2,1,0:T(8,128)(2,1)S(1)}, u32[]{:S(2)}, u32[]{:S(2)}) collective-permute-start(bf16[2,512,256]{2,1,0:T(8,128)(2,1)S(1)} %get-tuple-element.23.middle.own), channel_id=1, source_target_pairs={{0,5},{1,508},{2,7},{3,510},{4,9},{5,0},{6,11},{7,2},{8,13},{9,4},... | collective-permute-start | bytes 1572872 | tf_op jit(solution)/shard_map/ppermute | solution.py:226
  15.6 0.0 collective-permute-done.1.orbitals
  15.6 0.0 collective-permute-done.mate
  15.6 2.0 %edge_half.1 = (bf16[4,256,256]{2,1,0:T(8,128)(2,1)S(1)}, bf16[4,256,256]{2,1,0:T(8,128)(2,1)S(1)}, bf16[6,512,256]{2,1,0:T(8,128)(2,1)S(1)}) custom-call(s32[3,1,4]{2,1,0:T(1,128)} %bitcast.6, bf16[2,3,512,512]{3,2,1,0:T(8,128)(2,1)} %bitcast.4, bf16[2,512,512]{2,1,0:T(8,128)(2,1)S(1)} %collective-permute-done.mate, ...), custom_call_target="tpu_custom_call" | custom-call | flops 3000000000 | bytes 1 | tf_op jit(solution)/shard_map/edge_half/pallas_call | solution.py:17
  17.6 1.9 %collective-permute-start.4 = (bf16[6,512,256]{2,1,0:T(8,128)(2,1)S(1)}, bf16[6,512,256]{2,1,0:T(8,128)(2,1)S(1)}, u32[]{:S(2)}, u32[]{:S(2)}) collective-permute-start(bf16[6,512,256]{2,1,0:T(8,128)(2,1)S(1)} %get-tuple-element.26.mine), channel_id=1, source_target_pairs={{0,1},{1,0},{2,3},{3,2},{4,5},{5,4},{6,7},{7,6},{8,9},{9,8},{10,11... | collective-permute-start | bytes 4718600 | tf_op jit(solution)/shard_map/ppermute | solution.py:226
  19.5 3.8 %collective-permute-start.7 = (bf16[4,256,256]{2,1,0:T(8,128)(2,1)S(1)}, bf16[4,256,256]{2,1,0:T(8,128)(2,1)S(1)}, u32[]{:S(2)}, u32[]{:S(2)}) collective-permute-start(bf16[4,256,256]{2,1,0:T(8,128)(2,1)S(1)} %get-tuple-element.24.away), channel_id=1, source_target_pairs={{0,5},{1,508},{2,7},{3,510},{4,9},{5,0},{6,11},{7,2},{8,13},{9,4},... | collective-permute-start | bytes 1572872 | tf_op jit(solution)/shard_map/ppermute | solution.py:226
  23.3 3.9 %collective-permute-start.5 = (bf16[4,256,256]{2,1,0:T(8,128)(2,1)S(1)}, bf16[4,256,256]{2,1,0:T(8,128)(2,1)S(1)}, u32[]{:S(2)}, u32[]{:S(2)}) collective-permute-start(bf16[4,256,256]{2,1,0:T(8,128)(2,1)S(1)} %get-tuple-element.25.home), channel_id=1, source_target_pairs={{0,5},{1,508},{2,7},{3,510},{4,9},{5,0},{6,11},{7,2},{8,13},{9,4},... | collective-permute-start | bytes 1572872 | tf_op jit(solution)/shard_map/ppermute | solution.py:226
  27.2 0.0 collective-permute-done.3.near
  27.2 0.5 shared.1.part
  27.7 1.0 %diag.1 = f32[2,512,128]{2,1,0:T(8,128)S(1)} custom-call(bf16[6,512,256]{2,1,0:T(8,128)(2,1)S(1)} %get-tuple-element.26.mine, bf16[6,512,256]{2,1,0:T(8,128)(2,1)S(1)} %collective-permute-done.4.theirs.mate), custom_call_target="tpu_custom_call" | custom-call | flops 1 | bytes 1 | tf_op jit(solution)/shard_map/diag/pallas_call | solution.py:17
  28.8 4.1 %collective-permute-done.7.other = bf16[4,256,256]{2,1,0:T(8,128)(2,1)S(1)} collective-permute-done((bf16[4,256,256]{2,1,0:T(8,128)(2,1)S(1)}, bf16[4,256,256]{2,1,0:T(8,128)(2,1)S(1)}, u32[]{:S(2)}, u32[]{:S(2)}) %collective-permute-start.7) | collective-permute-done | bytes 524320 | tf_op jit(solution)/shard_map/ppermute | solution.py:226
  32.9 0.5 away.1
  33.3 4.0 %collective-permute-start.8 = (bf16[512,256]{1,0:T(8,128)(2,1)S(1)}, bf16[512,256]{1,0:T(8,128)(2,1)S(1)}, u32[]{:S(2)}, u32[]{:S(2)}) collective-permute-start(bf16[512,256]{1,0:T(8,128)(2,1)S(1)} %get-tuple-element.29), channel_id=1, source_target_pairs={{0,2},{1,3},{2,0},{3,1},{4,6},{5,7},{6,4},{7,5},{8,10},{9,11},{10,... | collective-permute-start | bytes 786440 | tf_op jit(solution)/shard_map/ppermute | solution.py:226
  37.4 1.9 %collective-permute-start.9 = (bf16[512,128]{1,0:T(8,128)(2,1)S(1)}, bf16[512,128]{1,0:T(8,128)(2,1)S(1)}, u32[]{:S(2)}, u32[]{:S(2)}) collective-permute-start(bf16[512,128]{1,0:T(8,128)(2,1)S(1)} %get-tuple-element.30), channel_id=1, source_target_pairs={{0,3},{1,2},{2,1},{3,0},{4,7},{5,6},{6,5},{7,4},{8,11},{9,10},{10,... | collective-permute-start | bytes 393224 | tf_op jit(solution)/shard_map/ppermute | solution.py:226
  39.3 0.0 collective-permute-done.5.other
  39.3 0.8 %home.1 = (f32[2,512,128]{2,1,0:T(8,128)S(1)}, f32[512,128]{1,0:T(8,128)S(1)}) custom-call(bf16[4,256,256]{2,1,0:T(8,128)(2,1)S(1)} %get-tuple-element.24.away, bf16[4,256,256]{2,1,0:T(8,128)(2,1)S(1)} %get-tuple-element.25.home, bf16[2,512,256]{2,1,0:T(8,128)(2,1)S(1)} %collective-permute-done.2.same, bf16[2,512,256]{2,1,0:T(8,128)(2,1)S(1)} %collective-permute-done.3.near, ...), custom_call_target="tpu_custom_call" | custom-call | flops 1 | bytes 1 | tf_op jit(solution)/shard_map/home/pallas_call | solution.py:17
  40.1 3.1 %collective-permute-start.6 = (f32[512,128]{1,0:T(8,128)S(1)}, f32[512,128]{1,0:T(8,128)S(1)}, u32[]{:S(2)}, u32[]{:S(2)}) collective-permute-start(f32[512,128]{1,0:T(8,128)S(1)} %get-tuple-element.27), channel_id=1, source_target_pairs={{0,1},{1,0},{2,3},{3,2},{4,5},{5,4},{6,7},{7,6},{8,9},{9,8},{10,11... | collective-permute-start | bytes 786440 | tf_op jit(solution)/shard_map/ppermute | solution.py:226
  43.3 16.0 %collective-permute-done.9.refs_2_ = bf16[512,128]{1,0:T(8,128)(2,1)S(1)} collective-permute-done((bf16[512,128]{1,0:T(8,128)(2,1)S(1)}, bf16[512,128]{1,0:T(8,128)(2,1)S(1)}, u32[]{:S(2)}, u32[]{:S(2)}) %collective-permute-start.9) | collective-permute-done | bytes 131104 | tf_op jit(solution)/shard_map/ppermute | solution.py:226
  59.3 0.1 settle.1
  59.4 0.9 %band.1 = f32[3,512,128]{2,1,0:T(8,128)} custom-call(f32[512,128]{1,0:T(8,128)S(1)} %collective-permute-done.6.refs_0_, bf16[512,128]{1,0:T(8,128)(2,1)S(1)} %get-tuple-element.31.refs_1_, f32[2,512,128]{2,1,0:T(8,128)S(1)} %get-tuple-element.32.refs_2_), custom_call_target="tpu_custom_call" | custom-call | flops 1 | bytes 1 | tf_op jit(solution)/shard_map/band/pallas_call | solution.py:17
  (4 shorter events, 0.0 us)
Async XLA Ops:
  2.0 13.5 %collective-permute-start = (bf16[2,512,512]{2,1,0:T(8,128)(2,1)S(1)}, bf16[2,512,512]{2,1,0:T(8,128)(2,1)S(1)}, u32[]{:S(2)}, u32[]{:S(2)}) collective-permute-start(bf16[2,512,512]{2,1,0:T(8,128)(2,1)S(1)} %get-tuple-element.21), channel_id=1, source_target_pairs={{0,1},{1,0},{2,3},{3,2},{4,5},{5,4},{6,7},{7,6},{8,9},{9,8},{10,11... | collective-permute-start | bytes 3145736 | tf_op jit(solution)/shard_map/ppermute | solution.py:226
  4.6 10.9 %collective-permute-start.1 = (bf16[512,256]{1,0:T(8,128)(2,1)S(1)}, bf16[512,256]{1,0:T(8,128)(2,1)S(1)}, u32[]{:S(2)}, u32[]{:S(2)}) collective-permute-start(bf16[512,256]{1,0:T(8,128)(2,1)S(1)} %get-tuple-element.22), channel_id=1, source_target_pairs={{0,5},{1,508},{2,7},{3,510},{4,9},{5,0},{6,11},{7,2},{8,13},{9,4},... | collective-permute-start | bytes 786440 | tf_op jit(solution)/shard_map/ppermute | solution.py:226
  9.6 17.6 %collective-permute-start.2 = (bf16[2,512,256]{2,1,0:T(8,128)(2,1)S(1)}, bf16[2,512,256]{2,1,0:T(8,128)(2,1)S(1)}, u32[]{:S(2)}, u32[]{:S(2)}) collective-permute-start(bf16[2,512,256]{2,1,0:T(8,128)(2,1)S(1)} %get-tuple-element.23.middle.own), channel_id=1, source_target_pairs={{0,508},{1,5},{2,510},{3,7},{4,0},{5,9},{6,2},{7,11},{8,4},{9,13},... | collective-permute-start | bytes 1572872 | tf_op jit(solution)/shard_map/ppermute | solution.py:226
  11.5 15.7 %collective-permute-start.3 = (bf16[2,512,256]{2,1,0:T(8,128)(2,1)S(1)}, bf16[2,512,256]{2,1,0:T(8,128)(2,1)S(1)}, u32[]{:S(2)}, u32[]{:S(2)}) collective-permute-start(bf16[2,512,256]{2,1,0:T(8,128)(2,1)S(1)} %get-tuple-element.23.middle.own), channel_id=1, source_target_pairs={{0,5},{1,508},{2,7},{3,510},{4,9},{5,0},{6,11},{7,2},{8,13},{9,4},... | collective-permute-start | bytes 1572872 | tf_op jit(solution)/shard_map/ppermute | solution.py:226
  17.6 10.2 %collective-permute-start.4 = (bf16[6,512,256]{2,1,0:T(8,128)(2,1)S(1)}, bf16[6,512,256]{2,1,0:T(8,128)(2,1)S(1)}, u32[]{:S(2)}, u32[]{:S(2)}) collective-permute-start(bf16[6,512,256]{2,1,0:T(8,128)(2,1)S(1)} %get-tuple-element.26.mine), channel_id=1, source_target_pairs={{0,1},{1,0},{2,3},{3,2},{4,5},{5,4},{6,7},{7,6},{8,9},{9,8},{10,11... | collective-permute-start | bytes 4718600 | tf_op jit(solution)/shard_map/ppermute | solution.py:226
  19.5 13.4 %collective-permute-start.7 = (bf16[4,256,256]{2,1,0:T(8,128)(2,1)S(1)}, bf16[4,256,256]{2,1,0:T(8,128)(2,1)S(1)}, u32[]{:S(2)}, u32[]{:S(2)}) collective-permute-start(bf16[4,256,256]{2,1,0:T(8,128)(2,1)S(1)} %get-tuple-element.24.away), channel_id=1, source_target_pairs={{0,5},{1,508},{2,7},{3,510},{4,9},{5,0},{6,11},{7,2},{8,13},{9,4},... | collective-permute-start | bytes 1572872 | tf_op jit(solution)/shard_map/ppermute | solution.py:226
  23.3 16.0 %collective-permute-start.5 = (bf16[4,256,256]{2,1,0:T(8,128)(2,1)S(1)}, bf16[4,256,256]{2,1,0:T(8,128)(2,1)S(1)}, u32[]{:S(2)}, u32[]{:S(2)}) collective-permute-start(bf16[4,256,256]{2,1,0:T(8,128)(2,1)S(1)} %get-tuple-element.25.home), channel_id=1, source_target_pairs={{0,5},{1,508},{2,7},{3,510},{4,9},{5,0},{6,11},{7,2},{8,13},{9,4},... | collective-permute-start | bytes 1572872 | tf_op jit(solution)/shard_map/ppermute | solution.py:226
  33.3 25.9 %collective-permute-start.8 = (bf16[512,256]{1,0:T(8,128)(2,1)S(1)}, bf16[512,256]{1,0:T(8,128)(2,1)S(1)}, u32[]{:S(2)}, u32[]{:S(2)}) collective-permute-start(bf16[512,256]{1,0:T(8,128)(2,1)S(1)} %get-tuple-element.29), channel_id=1, source_target_pairs={{0,2},{1,3},{2,0},{3,1},{4,6},{5,7},{6,4},{7,5},{8,10},{9,11},{10,... | collective-permute-start | bytes 786440 | tf_op jit(solution)/shard_map/ppermute | solution.py:226
  37.4 21.9 %collective-permute-start.9 = (bf16[512,128]{1,0:T(8,128)(2,1)S(1)}, bf16[512,128]{1,0:T(8,128)(2,1)S(1)}, u32[]{:S(2)}, u32[]{:S(2)}) collective-permute-start(bf16[512,128]{1,0:T(8,128)(2,1)S(1)} %get-tuple-element.30), channel_id=1, source_target_pairs={{0,3},{1,2},{2,1},{3,0},{4,7},{5,6},{6,5},{7,4},{8,11},{9,10},{10,... | collective-permute-start | bytes 393224 | tf_op jit(solution)/shard_map/ppermute | solution.py:226
  40.1 19.2 %collective-permute-start.6 = (f32[512,128]{1,0:T(8,128)S(1)}, f32[512,128]{1,0:T(8,128)S(1)}, u32[]{:S(2)}, u32[]{:S(2)}) collective-permute-start(f32[512,128]{1,0:T(8,128)S(1)} %get-tuple-element.27), channel_id=1, source_target_pairs={{0,1},{1,0},{2,3},{3,2},{4,5},{5,4},{6,7},{7,6},{8,9},{9,8},{10,11... | collective-permute-start | bytes 786440 | tf_op jit(solution)/shard_map/ppermute | solution.py:226

commit v5 on v4

--- a/solution.py
+++ b/solution.py
@@ -79,31 +79,41 @@
     return pl.ds(pl.multiple_of(part * size, size), size)
 
 
-def edge_kernel(
-    mask, own, mate, orbitals, middle, away, home, bundle, mask_ref, planes, sems
-):
-    core, far = sides()
+def near_kernel(mask, ints, orbitals, out, mask_ref, planes, sems):
+    core, _ = sides()
     side = 2 - 2 * core
-    per, rows, _ = planes.shape
-    mid = rows // 2
+    per = out.shape[0]
     copies = [
-        pltpu.make_async_copy(own.at[p, side], planes.at[p], sems.at[p]) for p in range(per)
+        pltpu.make_async_copy(ints.at[p, side], planes.at[p], sems.at[p]) for p in range(per)
     ]
     copies.append(pltpu.make_async_copy(mask, mask_ref, sems.at[per]))
     for copy in copies:
         copy.start()
     copies[per].wait()
-    for p in (*range(per, 2 * per), *range(per)):
-        if p < per:
-            copies[p].wait()
-        source = planes.at[p] if p < per else mate.at[p - per]
+    for p in range(per):
+        copies[p].wait()
+        out[p] = weighted(mask_ref, side, 0, planes.at[p], orbitals)
+
+
+def edge_kernel(mask, ready, planes, orbitals, middle, away, home, bundle, mask_ref, sem):
+    core, far = sides()
+    side = 2 - 2 * core
+    copy = pltpu.make_async_copy(mask, mask_ref, sem.at[0])
+    copy.start()
+    per, rows, _ = planes.shape
+    mid = rows // 2
+    for p in range(per):
+        bundle[p] = ready[p]
+        bundle[2 * per + p] = middle[p]
         for out, part in ((away, 1 - far), (home, far)):
-            plane = source.at[spot(part, mid)]
+            out[p] = ready[p, spot(part, mid), :]
+    copy.wait()
+    for p in range(per):
+        for out, part in ((away, 1 - far), (home, far)):
+            plane = planes.at[p, spot(part, mid)]
             half = weighted(mask_ref, side, 2 * part, plane, orbitals)
-            out[p] = half
-            bundle[p, spot(part, mid), :] = half
-    for p in range(per):
-        bundle[2 * per + p] = middle[p]
+            out[per + p] = half
+            bundle[per + p, spot(part, mid), :] = half
 
 
 def product(left, right):
@@ -256,17 +266,22 @@
     same = to_same(own_half)
     near = to_edge(own_half)
     part = jax.ShapeDtypeStruct((2 * per, mid, cols), BF16)
+    (ready,) = call(
+        near_kernel,
+        "near_half",
+        [HBM, HBM, VMEM],
+        [half],
+        (mask, ints, edge_coef),
+        [smem, planes, pltpu.SemaphoreType.DMA((per + 1,))],
+        cost=COSTS["near"],
+    )
     away, home, bundle = call(
         edge_kernel,
         "edge_half",
-        [HBM, HBM, VMEM, VMEM, VMEM],
+        [HBM] + [VMEM] * 4,
         [part, part, jax.ShapeDtypeStruct((3 * per, rows, cols), BF16)],
-        (mask, ints, mate_edges, edge_coef, own_half),
-        [
-            smem,
-            planes,
-            pltpu.SemaphoreType.DMA((per + 1,)),
-        ],
+        (mask, ready, mate_edges, edge_coef, own_half),
+        [smem, pltpu.SemaphoreType.DMA((1,))],
         cost=COSTS["edge"],
     )
     other_away = to_edge(away)
@@ -327,7 +342,7 @@
     return jnp.transpose(band, (1, 0, 2))
 
 
-COSTS = {"edge": 3e9, "diag": 1, "shared": 2e10, "away": 8e9, "home": 1, "settle": 8e9}
+COSTS = {"near": 1e10, "edge": 3e9, "diag": 1, "shared": 2e10, "away": 8e9, "home": 1, "settle": 8e9}
 
 
 def solution(mesh):

time: 60.7 us -> 60.5 us (level)
  the two profiles are of different devices: /device:TPU:3 before, /device:TPU:1 now
where the time goes in v5:
time: 60.5 us; the launch traced here: 60 us
  starting transfers between devices  45.2 us (75%)
  Pallas kernels  8.83 us (15%)
  waiting for transfers between devices  5.74 us (9%)
    ppermute x10, starting transfers between devices, moved(): return lax.ppermute(value, ('blk', 'aux'), pairs)  45.2 us
    pallas_call x9, Pallas kernels, call(): pl.pallas_call(kernel, in_specs=specs, out_specs=[VMEM] * len(outs) if ou...  8.83 us
    ppermute x10, waiting for transfers between devices, moved(): return lax.ppermute(value, ('blk', 'aux'), pairs)  5.74 us
  transfers between devices with their start and end apart: 10, of which 2 were waited for; matrix products, arithmetic and copies ran while one was open for 0% of the time, Pallas kernels for 10%

profile of v5, /device:TPU:1, one launch (start us, length us, event | category | flops | bytes accessed | tf_op | source)
XLA Modules:
  0.0 60.0 jit_solution(4015298621692668342)
XLA Ops:
  0.0 2.0 %own_middle.1 = (bf16[2,512,256]{2,1,0:T(8,128)(2,1)S(1)}, bf16[512,256]{1,0:T(8,128)(2,1)S(1)}, bf16[2,512,512]{2,1,0:T(8,128)(2,1)S(1)}) custom-call(s32[3,1,4]{2,1,0:T(1,128)} %bitcast.5, bf16[2,3,512,512]{3,2,1,0:T(8,128)(2,1)} %bitcast.3, bf16[512,256]{1,0:T(8,128)(2,1)} %orbitals.1), custom_call_target="tpu_custom_call" | custom-call | flops 1 | bytes 1 | tf_op jit(solution)/shard_map/own_middle/pallas_call | solution.py:17
  2.0 15.9 %collective-permute-start = (bf16[512,256]{1,0:T(8,128)(2,1)S(1)}, bf16[512,256]{1,0:T(8,128)(2,1)S(1)}, u32[]{:S(2)}, u32[]{:S(2)}) collective-permute-start(bf16[512,256]{1,0:T(8,128)(2,1)S(1)} %get-tuple-element.21), channel_id=1, source_target_pairs={{0,5},{1,508},{2,7},{3,510},{4,9},{5,0},{6,11},{7,2},{8,13},{9,4},... | collective-permute-start | bytes 786440 | tf_op jit(solution)/shard_map/ppermute | solution.py:236
  17.9 1.9 %collective-permute-start.1 = (bf16[2,512,512]{2,1,0:T(8,128)(2,1)S(1)}, bf16[2,512,512]{2,1,0:T(8,128)(2,1)S(1)}, u32[]{:S(2)}, u32[]{:S(2)}) collective-permute-start(bf16[2,512,512]{2,1,0:T(8,128)(2,1)S(1)} %get-tuple-element.22), channel_id=1, source_target_pairs={{0,1},{1,0},{2,3},{3,2},{4,5},{5,4},{6,7},{7,6},{8,9},{9,8},{10,11... | collective-permute-start | bytes 3145736 | tf_op jit(solution)/shard_map/ppermute | solution.py:236
  19.9 1.9 %collective-permute-start.2 = (bf16[2,512,256]{2,1,0:T(8,128)(2,1)S(1)}, bf16[2,512,256]{2,1,0:T(8,128)(2,1)S(1)}, u32[]{:S(2)}, u32[]{:S(2)}) collective-permute-start(bf16[2,512,256]{2,1,0:T(8,128)(2,1)S(1)} %get-tuple-element.23.middle.own), channel_id=1, source_target_pairs={{0,508},{1,5},{2,510},{3,7},{4,0},{5,9},{6,2},{7,11},{8,4},{9,13},... | collective-permute-start | bytes 1572872 | tf_op jit(solution)/shard_map/ppermute | solution.py:236
  21.8 4.7 %collective-permute-start.3 = (bf16[2,512,256]{2,1,0:T(8,128)(2,1)S(1)}, bf16[2,512,256]{2,1,0:T(8,128)(2,1)S(1)}, u32[]{:S(2)}, u32[]{:S(2)}) collective-permute-start(bf16[2,512,256]{2,1,0:T(8,128)(2,1)S(1)} %get-tuple-element.23.middle.own), channel_id=1, source_target_pairs={{0,5},{1,508},{2,7},{3,510},{4,9},{5,0},{6,11},{7,2},{8,13},{9,4},... | collective-permute-start | bytes 1572872 | tf_op jit(solution)/shard_map/ppermute | solution.py:236
  26.5 0.0 collective-permute-done.orbitals
  26.5 1.9 %near_half.1.ready = bf16[2,512,256]{2,1,0:T(8,128)(2,1)S(1)} custom-call(s32[3,1,4]{2,1,0:T(1,128)} %bitcast.6, bf16[2,3,512,512]{3,2,1,0:T(8,128)(2,1)} %bitcast.4, bf16[512,256]{1,0:T(8,128)(2,1)S(1)} %collective-permute-done.orbitals), custom_call_target="tpu_custom_call" | custom-call | flops 10000000000 | bytes 1 | tf_op jit(solution)/shard_map/near_half/pallas_call | solution.py:17
  28.4 0.0 collective-permute-done.1.planes
  28.4 1.1 %edge_half.1 = (bf16[4,256,256]{2,1,0:T(8,128)(2,1)S(1)}, bf16[4,256,256]{2,1,0:T(8,128)(2,1)S(1)}, bf16[6,512,256]{2,1,0:T(8,128)(2,1)S(1)}) custom-call(s32[3,1,4]{2,1,0:T(1,128)} %bitcast.7, bf16[2,512,256]{2,1,0:T(8,128)(2,1)S(1)} %near_half.1.ready, bf16[2,512,512]{2,1,0:T(8,128)(2,1)S(1)} %collective-permute-done.1.planes, ...), custom_call_target="tpu_custom_call" | custom-call | flops 3000000000 | bytes 1 | tf_op jit(solution)/shard_map/edge_half/pallas_call | solution.py:17
  29.6 1.9 %collective-permute-start.4 = (bf16[6,512,256]{2,1,0:T(8,128)(2,1)S(1)}, bf16[6,512,256]{2,1,0:T(8,128)(2,1)S(1)}, u32[]{:S(2)}, u32[]{:S(2)}) collective-permute-start(bf16[6,512,256]{2,1,0:T(8,128)(2,1)S(1)} %get-tuple-element.26.mine), channel_id=1, source_target_pairs={{0,1},{1,0},{2,3},{3,2},{4,5},{5,4},{6,7},{7,6},{8,9},{9,8},{10,11... | collective-permute-start | bytes 4718600 | tf_op jit(solution)/shard_map/ppermute | solution.py:236
  31.5 5.2 %collective-permute-start.7 = (bf16[4,256,256]{2,1,0:T(8,128)(2,1)S(1)}, bf16[4,256,256]{2,1,0:T(8,128)(2,1)S(1)}, u32[]{:S(2)}, u32[]{:S(2)}) collective-permute-start(bf16[4,256,256]{2,1,0:T(8,128)(2,1)S(1)} %get-tuple-element.24.away), channel_id=1, source_target_pairs={{0,5},{1,508},{2,7},{3,510},{4,9},{5,0},{6,11},{7,2},{8,13},{9,4},... | collective-permute-start | bytes 1572872 | tf_op jit(solution)/shard_map/ppermute | solution.py:236
  36.7 4.6 %collective-permute-start.5 = (bf16[4,256,256]{2,1,0:T(8,128)(2,1)S(1)}, bf16[4,256,256]{2,1,0:T(8,128)(2,1)S(1)}, u32[]{:S(2)}, u32[]{:S(2)}) collective-permute-start(bf16[4,256,256]{2,1,0:T(8,128)(2,1)S(1)} %get-tuple-element.25.home), channel_id=1, source_target_pairs={{0,5},{1,508},{2,7},{3,510},{4,9},{5,0},{6,11},{7,2},{8,13},{9,4},... | collective-permute-start | bytes 1572872 | tf_op jit(solution)/shard_map/ppermute | solution.py:236
  41.3 0.5 shared.1.part
  41.9 1.0 %diag.1 = f32[2,512,128]{2,1,0:T(8,128)S(1)} custom-call(bf16[6,512,256]{2,1,0:T(8,128)(2,1)S(1)} %get-tuple-element.26.mine, bf16[6,512,256]{2,1,0:T(8,128)(2,1)S(1)} %collective-permute-done.4.theirs.mate), custom_call_target="tpu_custom_call" | custom-call | flops 1 | bytes 1 | tf_op jit(solution)/shard_map/diag/pallas_call | solution.py:17
  42.9 3.5 %collective-permute-done.7.other = bf16[4,256,256]{2,1,0:T(8,128)(2,1)S(1)} collective-permute-done((bf16[4,256,256]{2,1,0:T(8,128)(2,1)S(1)}, bf16[4,256,256]{2,1,0:T(8,128)(2,1)S(1)}, u32[]{:S(2)}, u32[]{:S(2)}) %collective-permute-start.7) | collective-permute-done | bytes 524320 | tf_op jit(solution)/shard_map/ppermute | solution.py:236
  46.3 0.5 away.1
  46.8 4.4 %collective-permute-start.8 = (bf16[512,256]{1,0:T(8,128)(2,1)S(1)}, bf16[512,256]{1,0:T(8,128)(2,1)S(1)}, u32[]{:S(2)}, u32[]{:S(2)}) collective-permute-start(bf16[512,256]{1,0:T(8,128)(2,1)S(1)} %get-tuple-element.29), channel_id=1, source_target_pairs={{0,2},{1,3},{2,0},{3,1},{4,6},{5,7},{6,4},{7,5},{8,10},{9,11},{10,... | collective-permute-start | bytes 786440 | tf_op jit(solution)/shard_map/ppermute | solution.py:236
  51.2 1.9 %collective-permute-start.9 = (bf16[512,128]{1,0:T(8,128)(2,1)S(1)}, bf16[512,128]{1,0:T(8,128)(2,1)S(1)}, u32[]{:S(2)}, u32[]{:S(2)}) collective-permute-start(bf16[512,128]{1,0:T(8,128)(2,1)S(1)} %get-tuple-element.30), channel_id=1, source_target_pairs={{0,3},{1,2},{2,1},{3,0},{4,7},{5,6},{6,5},{7,4},{8,11},{9,10},{10,... | collective-permute-start | bytes 393224 | tf_op jit(solution)/shard_map/ppermute | solution.py:236
  53.1 0.8 %home.1 = (f32[2,512,128]{2,1,0:T(8,128)S(1)}, f32[512,128]{1,0:T(8,128)S(1)}) custom-call(bf16[4,256,256]{2,1,0:T(8,128)(2,1)S(1)} %get-tuple-element.24.away, bf16[4,256,256]{2,1,0:T(8,128)(2,1)S(1)} %get-tuple-element.25.home, bf16[2,512,256]{2,1,0:T(8,128)(2,1)S(1)} %collective-permute-done.2.same, bf16[2,512,256]{2,1,0:T(8,128)(2,1)S(1)} %collective-permute-done.3.near, ...), custom_call_target="tpu_custom_call" | custom-call | flops 1 | bytes 1 | tf_op jit(solution)/shard_map/home/pallas_call | solution.py:17
  53.9 2.8 %collective-permute-start.6 = (f32[512,128]{1,0:T(8,128)S(1)}, f32[512,128]{1,0:T(8,128)S(1)}, u32[]{:S(2)}, u32[]{:S(2)}) collective-permute-start(f32[512,128]{1,0:T(8,128)S(1)} %get-tuple-element.27), channel_id=1, source_target_pairs={{0,1},{1,0},{2,3},{3,2},{4,5},{5,4},{6,7},{7,6},{8,9},{9,8},{10,11... | collective-permute-start | bytes 786440 | tf_op jit(solution)/shard_map/ppermute | solution.py:236
  56.7 2.2 %collective-permute-done.9.refs_2_ = bf16[512,128]{1,0:T(8,128)(2,1)S(1)} collective-permute-done((bf16[512,128]{1,0:T(8,128)(2,1)S(1)}, bf16[512,128]{1,0:T(8,128)(2,1)S(1)}, u32[]{:S(2)}, u32[]{:S(2)}) %collective-permute-start.9) | collective-permute-done | bytes 131104 | tf_op jit(solution)/shard_map/ppermute | solution.py:236
  59.0 0.1 settle.1
  59.1 0.0 collective-permute-done.6.refs_0_
  59.1 0.9 %band.1 = f32[3,512,128]{2,1,0:T(8,128)} custom-call(f32[512,128]{1,0:T(8,128)S(1)} %collective-permute-done.6.refs_0_, bf16[512,128]{1,0:T(8,128)(2,1)S(1)} %get-tuple-element.31.refs_1_, f32[2,512,128]{2,1,0:T(8,128)S(1)} %get-tuple-element.32.refs_2_), custom_call_target="tpu_custom_call" | custom-call | flops 1 | bytes 1 | tf_op jit(solution)/shard_map/band/pallas_call | solution.py:17
  (5 shorter events, 0.0 us)
Async XLA Ops:
  2.0 24.5 %collective-permute-start = (bf16[512,256]{1,0:T(8,128)(2,1)S(1)}, bf16[512,256]{1,0:T(8,128)(2,1)S(1)}, u32[]{:S(2)}, u32[]{:S(2)}) collective-permute-start(bf16[512,256]{1,0:T(8,128)(2,1)S(1)} %get-tuple-element.21), channel_id=1, source_target_pairs={{0,5},{1,508},{2,7},{3,510},{4,9},{5,0},{6,11},{7,2},{8,13},{9,4},... | collective-permute-start | bytes 786440 | tf_op jit(solution)/shard_map/ppermute | solution.py:236
  17.9 10.5 %collective-permute-start.1 = (bf16[2,512,512]{2,1,0:T(8,128)(2,1)S(1)}, bf16[2,512,512]{2,1,0:T(8,128)(2,1)S(1)}, u32[]{:S(2)}, u32[]{:S(2)}) collective-permute-start(bf16[2,512,512]{2,1,0:T(8,128)(2,1)S(1)} %get-tuple-element.22), channel_id=1, source_target_pairs={{0,1},{1,0},{2,3},{3,2},{4,5},{5,4},{6,7},{7,6},{8,9},{9,8},{10,11... | collective-permute-start | bytes 3145736 | tf_op jit(solution)/shard_map/ppermute | solution.py:236
  19.9 21.5 %collective-permute-start.2 = (bf16[2,512,256]{2,1,0:T(8,128)(2,1)S(1)}, bf16[2,512,256]{2,1,0:T(8,128)(2,1)S(1)}, u32[]{:S(2)}, u32[]{:S(2)}) collective-permute-start(bf16[2,512,256]{2,1,0:T(8,128)(2,1)S(1)} %get-tuple-element.23.middle.own), channel_id=1, source_target_pairs={{0,508},{1,5},{2,510},{3,7},{4,0},{5,9},{6,2},{7,11},{8,4},{9,13},... | collective-permute-start | bytes 1572872 | tf_op jit(solution)/shard_map/ppermute | solution.py:236
  21.8 19.6 %collective-permute-start.3 = (bf16[2,512,256]{2,1,0:T(8,128)(2,1)S(1)}, bf16[2,512,256]{2,1,0:T(8,128)(2,1)S(1)}, u32[]{:S(2)}, u32[]{:S(2)}) collective-permute-start(bf16[2,512,256]{2,1,0:T(8,128)(2,1)S(1)} %get-tuple-element.23.middle.own), channel_id=1, source_target_pairs={{0,5},{1,508},{2,7},{3,510},{4,9},{5,0},{6,11},{7,2},{8,13},{9,4},... | collective-permute-start | bytes 1572872 | tf_op jit(solution)/shard_map/ppermute | solution.py:236
  29.6 12.2 %collective-permute-start.4 = (bf16[6,512,256]{2,1,0:T(8,128)(2,1)S(1)}, bf16[6,512,256]{2,1,0:T(8,128)(2,1)S(1)}, u32[]{:S(2)}, u32[]{:S(2)}) collective-permute-start(bf16[6,512,256]{2,1,0:T(8,128)(2,1)S(1)} %get-tuple-element.26.mine), channel_id=1, source_target_pairs={{0,1},{1,0},{2,3},{3,2},{4,5},{5,4},{6,7},{7,6},{8,9},{9,8},{10,11... | collective-permute-start | bytes 4718600 | tf_op jit(solution)/shard_map/ppermute | solution.py:236
  31.5 14.8 %collective-permute-start.7 = (bf16[4,256,256]{2,1,0:T(8,128)(2,1)S(1)}, bf16[4,256,256]{2,1,0:T(8,128)(2,1)S(1)}, u32[]{:S(2)}, u32[]{:S(2)}) collective-permute-start(bf16[4,256,256]{2,1,0:T(8,128)(2,1)S(1)} %get-tuple-element.24.away), channel_id=1, source_target_pairs={{0,5},{1,508},{2,7},{3,510},{4,9},{5,0},{6,11},{7,2},{8,13},{9,4},... | collective-permute-start | bytes 1572872 | tf_op jit(solution)/shard_map/ppermute | solution.py:236
  36.7 16.4 %collective-permute-start.5 = (bf16[4,256,256]{2,1,0:T(8,128)(2,1)S(1)}, bf16[4,256,256]{2,1,0:T(8,128)(2,1)S(1)}, u32[]{:S(2)}, u32[]{:S(2)}) collective-permute-start(bf16[4,256,256]{2,1,0:T(8,128)(2,1)S(1)} %get-tuple-element.25.home), channel_id=1, source_target_pairs={{0,5},{1,508},{2,7},{3,510},{4,9},{5,0},{6,11},{7,2},{8,13},{9,4},... | collective-permute-start | bytes 1572872 | tf_op jit(solution)/shard_map/ppermute | solution.py:236
  46.8 12.2 %collective-permute-start.8 = (bf16[512,256]{1,0:T(8,128)(2,1)S(1)}, bf16[512,256]{1,0:T(8,128)(2,1)S(1)}, u32[]{:S(2)}, u32[]{:S(2)}) collective-permute-start(bf16[512,256]{1,0:T(8,128)(2,1)S(1)} %get-tuple-element.29), channel_id=1, source_target_pairs={{0,2},{1,3},{2,0},{3,1},{4,6},{5,7},{6,4},{7,5},{8,10},{9,11},{10,... | collective-permute-start | bytes 786440 | tf_op jit(solution)/shard_map/ppermute | solution.py:236
  51.2 7.8 %collective-permute-start.9 = (bf16[512,128]{1,0:T(8,128)(2,1)S(1)}, bf16[512,128]{1,0:T(8,128)(2,1)S(1)}, u32[]{:S(2)}, u32[]{:S(2)}) collective-permute-start(bf16[512,128]{1,0:T(8,128)(2,1)S(1)} %get-tuple-element.30), channel_id=1, source_target_pairs={{0,3},{1,2},{2,1},{3,0},{4,7},{5,6},{6,5},{7,4},{8,11},{9,10},{10,... | collective-permute-start | bytes 393224 | tf_op jit(solution)/shard_map/ppermute | solution.py:236
  53.9 5.1 %collective-permute-start.6 = (f32[512,128]{1,0:T(8,128)S(1)}, f32[512,128]{1,0:T(8,128)S(1)}, u32[]{:S(2)}, u32[]{:S(2)}) collective-permute-start(f32[512,128]{1,0:T(8,128)S(1)} %get-tuple-element.27), channel_id=1, source_target_pairs={{0,1},{1,0},{2,3},{3,2},{4,5},{5,4},{6,7},{7,6},{8,9},{9,8},{10,11... | collective-permute-start | bytes 786440 | tf_op jit(solution)/shard_map/ppermute | solution.py:236
